TPU v7x, 256 devices: a whole 4x4x8 slice. The times are simulated.
256 devices in a mesh: tx: 8 (over z), ty: 2 (over y_lo), vel: 16 (over x, y_hi, core).
Axes of the slice: x: 4, y: 4 (y_hi: 2, y_lo: 2; y = y_hi * 2 + y_lo), z: 8, core: 2. Of those that a mesh axis runs over, the one named last changes fastest.
Arguments:
- initial: float32 [64, 16, 16, 12288], P('tx', 'ty', None, 'vel'), may hold values from -2 to 3.5
- velocity: float32 [3, 12288], P(None, 'vel'), may hold values from -3 to 3, as said below
- weights: float32 [12288], P('vel'), may hold values from 0.5 to 2
- wall: int32 [64, 16, 16], P('tx', 'ty'), may hold values 0 or 1
- wall_temp: float32 [64, 16, 16], P('tx', 'ty'), may hold values from -1 to 1
- mass_target: float32 [], replicated, may hold values from 0.5 to 1.5
Outputs:
- distribution: float32 [64, 16, 16, 12288], P('tx', 'ty', None, 'vel')
- macro_fields: float32 [5, 64, 16, 16], P(None, 'tx', 'ty')
Inputs may be any that keep to these rules, and one draw needn't show every extreme that they name: `velocity`: within each aligned block of 768 velocities the first quarter has positive x and y components, the second positive x and negative y, the third negative x and positive y, the fourth negative x and y; x and y components are 0.05 or more in magnitude.
All inputs are finite; a program needn't handle non-finite values. No bound on the sum of `wall` on one device may be relied on, other than what follows from the above.
Results may differ from a plain program's by a relative error of at most 0.0003.
Values sent between devices are 32-bit elements; how exact they have to be, the bound alone decides.
A program may use at most 128 MiB of HBM per device.

v0:
```python
import jax
import jax.numpy as jnp
from jax import lax
from jax.sharding import PartitionSpec as P

ITERS = 3
MACRO_STEPS = 4


step_time = 0.1
collision = 1.0
macro_time = 0.1
viscosity = 1.0
conduction = 1.0
highest = lax.Precision.HIGHEST


def extended(value, sides, width):
    edges = {}
    for axis, dim in sides:
        count, length = (lax.axis_size(axis), value.shape[dim])
        up = [(i, (i + 1) % count) for i in range(count)]
        last = lax.slice_in_dim(value, length - width, length, axis=dim)
        first = lax.slice_in_dim(value, 0, width, axis=dim)
        edges[dim] = (
            lax.ppermute(last, axis, up),
            lax.ppermute(first, axis, [(b, a) for a, b in up]),
        )
    done = []
    for _, dim in sides:
        low, high = edges[dim]
        around = [(width, width) if d in done else (0, 0) for d in range(value.ndim)]
        value = jnp.concatenate([jnp.pad(low, around), value, jnp.pad(high, around)], axis=dim)
        done.append(dim)
    return value


def from_everyone(value, axis):
    copies = jnp.broadcast_to(value, (lax.axis_size(axis), *value.shape))
    return lax.all_to_all(copies, axis, split_axis=0, concat_axis=0, tiled=True)


def over_copies(value, axis):
    return from_everyone(value, axis).sum(axis=0)


def basis(velocity):
    speed_sq = velocity[0] * velocity[0] + velocity[1] * velocity[1] + velocity[2] * velocity[2]
    return jnp.stack(
        [
            jnp.ones_like(speed_sq),
            2.0 * velocity[0],
            2.0 * velocity[1],
            2.0 * velocity[2],
            speed_sq - 1.5,
        ]
    )


def projector(velocity, weights, total_count):
    vel_x, vel_y, vel_z = (velocity[0], velocity[1], velocity[2])
    speed_sq = vel_x * vel_x + vel_y * vel_y + vel_z * vel_z
    moment_rows = jnp.stack(
        [
            jnp.ones_like(speed_sq),
            vel_x,
            vel_y,
            vel_z,
            2.0 / 3.0 * speed_sq - 1.0,
            2.0 * (vel_x * vel_x - speed_sq / 3.0),
            2.0 * (vel_y * vel_y - speed_sq / 3.0),
            2.0 * (vel_z * vel_z - speed_sq / 3.0),
            2.0 * vel_x * vel_y,
            2.0 * vel_x * vel_z,
            2.0 * vel_y * vel_z,
            vel_x * (speed_sq - 2.5),
            vel_y * (speed_sq - 2.5),
            vel_z * (speed_sq - 2.5),
        ]
    )
    return moment_rows * (weights / total_count)[None, :]


def differences(shifted):
    grads = [(shifted(direction, 1) - shifted(direction, -1)) * 0.5 for direction in (1, 2, 3)]
    middle = shifted(1, 0)
    laplace = (
        shifted(1, 1)
        + shifted(1, -1)
        - 2.0 * middle
        + (shifted(2, 1) + shifted(2, -1) - 2.0 * middle)
    )
    laplace = laplace + (shifted(3, 1) + shifted(3, -1) - 2.0 * middle)
    return (grads, laplace, middle)


def macro_sources(shifted):
    grads, laplace, middle = differences(shifted)
    grad_x, grad_y, grad_z = grads
    sig_x = grad_x[0] + grad_y[3] + grad_z[4]
    sig_y = grad_x[3] + grad_y[1] + grad_z[5]
    sig_z = grad_x[4] + grad_y[5] + grad_z[2]
    heat_flow = grad_x[6] + grad_y[7] + grad_z[8]
    return jnp.stack(
        [
            -0.5 * (sig_x + viscosity * laplace[9]),
            -0.5 * (sig_y + viscosity * laplace[10]),
            -0.5 * (sig_z + viscosity * laplace[11]),
            -(2.0 / 3.0) * (heat_flow + conduction * laplace[12]),
        ]
    )


def macro_step(shifted, sources):
    grads, laplace, middle = differences(shifted)
    grad_x, grad_y, grad_z = grads
    div_u = grad_x[1] + grad_y[2] + grad_z[3]
    change_rates = [-div_u]
    for component in range(3):
        along = grads[component]
        change_rates.append(
            -0.5 * (along[0] + along[4])
            + 0.5 * viscosity * laplace[1 + component]
            + sources[component]
        )
    change_rates.append(-(2.0 / 3.0) * div_u + 2.0 / 3.0 * conduction * laplace[4] + sources[3])
    return middle + macro_time * jnp.stack(change_rates)


def kinetic_update(corrected, equilibrium, before_x, after_x, before_y, after_y, velocity):
    plus_part = jnp.maximum(velocity, 0.0)
    minus_part = jnp.minimum(velocity, 0.0)
    before_z = jnp.roll(corrected, 1, 2)
    after_z = jnp.roll(corrected, -1, 2)
    transport = plus_part[0] * (corrected - before_x) + minus_part[0] * (after_x - corrected)
    transport = transport + (
        plus_part[1] * (corrected - before_y) + minus_part[1] * (after_y - corrected)
    )
    transport = transport + (
        plus_part[2] * (corrected - before_z) + minus_part[2] * (after_z - corrected)
    )
    return corrected - step_time * transport + step_time * collision * (equilibrium - corrected)


def padded_view(padded):

    def shifted(direction, offset):
        selector = [slice(None), slice(1, -1), slice(1, -1), slice(1, -1)]
        extent = padded.shape[direction]
        selector[direction] = slice(1 + offset, extent - 1 + offset)
        return padded[tuple(selector)]

    return shifted


def wrap_depth(padded):
    return jnp.concatenate([padded[..., -1:], padded, padded[..., :1]], axis=3)


def pad_sources(fields):
    padded = wrap_depth(extended(fields, (("tx", 1), ("ty", 2)), 1))
    return padded


def pad_state(macro_state):
    padded = wrap_depth(extended(macro_state, (("tx", 1), ("ty", 2)), 1))
    return padded


def total_mass(local_sum):
    summed = over_copies(local_sum, ("tx", "ty"))
    return summed


def on_device(initial, velocity, weights, wall, wall_temp, mass_target):
    width_dev = weights.shape[0]
    total_velocities = float(width_dev * lax.axis_size("vel"))
    cell_count = float(
        wall.shape[0] * wall.shape[1] * wall.shape[2] * lax.axis_size("tx") * lax.axis_size("ty")
    )
    moment_rows = projector(velocity, weights, total_velocities)
    rows = basis(velocity)
    is_wall = (wall == 1)[..., None]
    wall_state = wall_temp[..., None] * rows[4]
    distribution = initial
    macro_state = None
    for iteration in range(ITERS):
        local_moments = jnp.einsum("kv,xyzv->kxyz", moment_rows, distribution, precision=highest)
        moments = over_copies(local_moments, "vel")
        kinetic_state = moments[0:5]
        fields = jnp.concatenate([moments[5:14], moments[1:5]])
        mass_total = total_mass(jnp.sum(kinetic_state[0]))
        sources = macro_sources(padded_view(pad_sources(fields)))
        macro_state = kinetic_state
        for sweep in range(MACRO_STEPS):
            macro_state = macro_step(padded_view(pad_state(macro_state)), sources)
        density_mean = mass_total / cell_count
        macro_state = jnp.concatenate(
            [(macro_state[0] - density_mean + mass_target)[None], macro_state[1:]]
        )
        change = macro_state - kinetic_state
        corrected = distribution + jnp.einsum("kxyz,kv->xyzv", change, rows, precision=highest)
        equilibrium = jnp.einsum("kxyz,kv->xyzv", macro_state, rows, precision=highest)
        padded = extended(corrected, (("tx", 0), ("ty", 1)), 1)
        before_x = padded[:-2, 1:-1]
        after_x = padded[2:, 1:-1]
        before_y = padded[1:-1, :-2]
        after_y = padded[1:-1, 2:]
        updated = kinetic_update(
            corrected, equilibrium, before_x, after_x, before_y, after_y, velocity
        )
        distribution = jnp.where(is_wall, wall_state, updated)
    return (distribution, macro_state)


def solution(mesh):
    placed = (
        P("tx", "ty", None, "vel"),
        P(None, "vel"),
        P("vel"),
        P("tx", "ty", None),
        P("tx", "ty", None),
        P(),
    )
    return jax.shard_map(
        on_device,
        mesh=mesh,
        in_specs=placed,
        out_specs=(P("tx", "ty", None, "vel"), P(None, "tx", "ty", None)),
        check_vma=False,
    )
```

profile of v0, /device:TPU:8, one launch (start us, length us, event | category | flops | bytes accessed | tf_op | source)
XLA Modules:
  0.0 436.0 jit_solution(18194794890388194346)
XLA Ops:
  3.8 12.9 %fusion.85 = f32[14,8,8,16]{3,0,2,1:T(8,128)S(1)} fusion(f32[8,8,16,768]{3,2,1,0:T(8,128)} %param.6, f32[14,768]{1,0:T(8,128)S(1)} %stack.29, f32[768]{0:T(1024)S(1)} %broadcast_multiply_fusion), kind=kOutput, calls=%fused_computation.588 | convolution fusion | flops 132131328 | bytes 3249152 | tf_op jit(solution)/shard_map/kv,xyzv->kxyz/dot_general | solution.py:188
  16.9 4.0 broadcast_in_dim.39
  20.9 5.9 %reshape.53 = f32[16,1,14336]{2,1,0:T(1,128)} reshape(f32[16,14,8,8,16]{4,3,2,1,0:T(8,128)} %broadcast_in_dim.39) | data formatting | bytes 1835008
  26.8 6.4 %all-to-all-start = ((f32[16,1,14336]{2,1,0:T(1,128)}), f32[16,1,14336]{2,1,0:T(1,128)S(1)}, u32[]{:S(2)}, u32[]{:S(2)}) async-start(f32[16,1,14336]{2,1,0:T(1,128)} %reshape.53), calls=%async_computation | async-start | bytes 1835008 | tf_op jit(solution)/shard_map/all_to_all | solution.py:40
  33.3 16.5 %all-to-all-done = f32[16,1,14336]{2,1,0:T(1,128)S(1)} async-done(((f32[16,1,14336]{2,1,0:T(1,128)}), f32[16,1,14336]{2,1,0:T(1,128)S(1)}, u32[]{:S(2)}, u32[]{:S(2)}) %all-to-all-start) | async-done | bytes 917536 | tf_op jit(solution)/shard_map/all_to_all | solution.py:40
  50.3 2.8 reduce.20
  53.1 4.4 %reshape.54 = f32[16,14,8,8,16]{4,3,2,1,0:T(8,128)} reshape(f32[16,14336]{1,0:T(8,128)S(1)} %reduce.20) | data formatting | bytes 1835008
  57.5 4.0 reduce_sum.81
  63.7 1.9 collective-permute-start.1
  65.6 3.9 collective-permute-start
  69.8 3.2 collective-permute-start.4
  77.3 1.9 collective-permute-done.6
  83.9 3.2 collective-permute-start.8
  87.2 1.7 collective-permute-done.9
  92.1 3.2 collective-permute-start.12
  100.4 3.3 collective-permute-start.17
  106.0 7.2 %all-to-all-start.1 = ((f32[16,1,1]{2,1,0:T(1,128)}), f32[16,1,1]{2,1,0:T(1,128)S(1)}, u32[]{:S(2)}, u32[]{:S(2)}) async-start(f32[16,1,1]{2,1,0:T(1,128)} %broadcast_in_dim.40), calls=%async_computation.1 | async-start | bytes 16384 | tf_op jit(solution)/shard_map/all_to_all | solution.py:40
  113.3 7.0 %all-to-all-done.1 = f32[16,1,1]{2,1,0:T(1,128)S(1)} async-done(((f32[16,1,1]{2,1,0:T(1,128)}), f32[16,1,1]{2,1,0:T(1,128)S(1)}, u32[]{:S(2)}, u32[]{:S(2)}) %all-to-all-start.1) | async-done | bytes 96 | tf_op jit(solution)/shard_map/all_to_all | solution.py:40
  123.7 2.8 convolution_add_fusion.2
  129.6 2.9 collective-permute-start.21
  133.0 1.7 collective-permute-done.22
  134.8 4.2 collective-permute-done.23
  139.1 6.1 %multiply_select_fusion.2 = f32[8,8,16,768]{3,2,1,0:T(8,128)S(1)} fusion(f32[8,8,16,768]{3,2,1,0:T(8,128)S(1)} %convolution_add_fusion.2, f32[8,1,16,768]{3,2,1,0:T(8,128)S(1)} %collective-permute-done.23, f32[1,8,16,768]{3,2,1,0:T(8,128)S(1)} %collective-permute-done.21, f32[1,8,16,768]{3,2,1,0:T(8,128)S(1)} %collective-permute-done.20, ...), kind=kOutput, calls=%fused_computation.2 | convolution fusion | flops 78643200 | bytes 14218240 | tf_op jit(solution)/shard_map/kxyz,kv->xyzv/dot_general | solution.py:203
  145.2 11.5 %fusion.83 = f32[14,8,8,16]{3,0,2,1:T(8,128)S(1)} fusion(f32[8,8,16,768]{3,2,1,0:T(8,128)S(1)} %multiply_select_fusion.2, f32[14,768]{1,0:T(8,128)S(1)} %stack.29, f32[768]{0:T(1024)S(1)} %broadcast_multiply_fusion), kind=kOutput, calls=%fused_computation.586 | convolution fusion | flops 132131328 | bytes 3249152 | tf_op jit(solution)/shard_map/kv,xyzv->kxyz/dot_general | solution.py:188
  156.9 4.0 broadcast_in_dim.41
  160.8 5.9 %reshape.55 = f32[16,1,14336]{2,1,0:T(1,128)} reshape(f32[16,14,8,8,16]{4,3,2,1,0:T(8,128)} %broadcast_in_dim.41) | data formatting | bytes 1835008
  166.7 20.7 %all_to_all.33 = f32[16,1,14336]{2,1,0:T(1,128)} all-to-all(f32[16,1,14336]{2,1,0:T(1,128)} %reshape.55), channel_id=1, replica_groups=mesh['tx'=8,'ty'=2,'vel'=16] {'vel'}, dimensions={0} | all-to-all | bytes 1835008 | tf_op jit(solution)/shard_map/all_to_all | solution.py:40
  187.4 4.9 %reduce.21 = f32[16,14336]{1,0:T(8,128)} reduce(f32[16,1,14336]{2,1,0:T(1,128)} %all_to_all.33, f32[]{:T(128)} %broadcast.599), dimensions={1}, to_apply=%all_to_all.23.reduce_sub_computation | reduce | bytes 1835012 | tf_op jit(solution)/shard_map/all_to_all | solution.py:40
  192.3 5.4 %reshape.56 = f32[16,14,8,8,16]{4,3,2,1,0:T(8,128)} reshape(f32[16,14336]{1,0:T(8,128)} %reduce.21) | data formatting | bytes 1835008
  197.7 4.8 %reduce_sum.84 = f32[14,8,8,16]{3,2,1,0:T(8,128)} reduce(f32[16,14,8,8,16]{4,3,2,1,0:T(8,128)} %reshape.56, f32[]{:T(128)} %constant.10.clone.1), dimensions={0}, to_apply=%region_3.4 | reduce | flops 215040 | bytes 974852 | tf_op jit(solution)/shard_map/reduce_sum | solution.py:44
  208.8 2.7 collective-permute-start.24
  212.6 3.2 collective-permute-start.28
  215.8 1.7 collective-permute-start.31
  227.3 3.2 collective-permute-start.32
  230.6 1.7 collective-permute-done.33
  235.6 3.2 collective-permute-start.36
  238.9 1.7 collective-permute-done.37
  245.2 3.2 collective-permute-start.40
  250.5 12.0 %all_to_all.34 = f32[16,1,1]{2,1,0:T(1,128)} all-to-all(f32[16,1,1]{2,1,0:T(1,128)S(1)} %broadcast_in_dim.42), channel_id=1, replica_groups=mesh['tx'=8,'ty'=2,'vel'=16] {'tx','ty'}, dimensions={0} | all-to-all | bytes 128 | tf_op jit(solution)/shard_map/all_to_all | solution.py:40
  268.3 2.8 convolution_add_fusion.1
  274.2 3.2 collective-permute-start.45
  279.4 4.2 collective-permute-done.47
  283.7 6.1 %multiply_select_fusion.1 = f32[8,8,16,768]{3,2,1,0:T(8,128)S(1)} fusion(f32[8,8,16,768]{3,2,1,0:T(8,128)S(1)} %convolution_add_fusion.1, f32[8,1,16,768]{3,2,1,0:T(8,128)S(1)} %collective-permute-done.47, f32[1,8,16,768]{3,2,1,0:T(8,128)S(1)} %collective-permute-done.45, f32[1,8,16,768]{3,2,1,0:T(8,128)S(1)} %collective-permute-done.44, ...), kind=kOutput, calls=%fused_computation.1 | convolution fusion | flops 78643200 | bytes 14218240 | tf_op jit(solution)/shard_map/kxyz,kv->xyzv/dot_general | solution.py:203
  289.8 11.2 %fusion.81 = f32[14,8,8,16]{3,0,2,1:T(8,128)S(1)} fusion(f32[8,8,16,768]{3,2,1,0:T(8,128)S(1)} %multiply_select_fusion.1, f32[14,768]{1,0:T(8,128)S(1)} %stack.29, f32[768]{0:T(1024)S(1)} %copy-done.4), kind=kOutput, calls=%fused_computation.584 | convolution fusion | flops 132131328 | bytes 3249152 | tf_op jit(solution)/shard_map/kv,xyzv->kxyz/dot_general | solution.py:188
  301.2 4.0 broadcast_in_dim.43
  305.1 5.9 %reshape.57 = f32[16,1,14336]{2,1,0:T(1,128)} reshape(f32[16,14,8,8,16]{4,3,2,1,0:T(8,128)} %broadcast_in_dim.43) | data formatting | bytes 1835008
  311.0 20.7 %all_to_all.35 = f32[16,1,14336]{2,1,0:T(1,128)} all-to-all(f32[16,1,14336]{2,1,0:T(1,128)} %reshape.57), channel_id=1, replica_groups=mesh['tx'=8,'ty'=2,'vel'=16] {'vel'}, dimensions={0} | all-to-all | bytes 1835008 | tf_op jit(solution)/shard_map/all_to_all | solution.py:40
  331.7 4.9 %reduce.22 = f32[16,14336]{1,0:T(8,128)} reduce(f32[16,1,14336]{2,1,0:T(1,128)} %all_to_all.35, f32[]{:T(128)} %broadcast.599), dimensions={1}, to_apply=%all_to_all.25.reduce_sub_computation | reduce | bytes 1835012 | tf_op jit(solution)/shard_map/all_to_all | solution.py:40
  336.6 5.4 %reshape.58 = f32[16,14,8,8,16]{4,3,2,1,0:T(8,128)} reshape(f32[16,14336]{1,0:T(8,128)} %reduce.22) | data formatting | bytes 1835008
  342.0 4.8 %reduce_sum.87 = f32[14,8,8,16]{3,2,1,0:T(8,128)} reduce(f32[16,14,8,8,16]{4,3,2,1,0:T(8,128)} %reshape.58, f32[]{:T(128)} %constant.10.clone.1), dimensions={0}, to_apply=%region_6.7 | reduce | flops 215040 | bytes 974852 | tf_op jit(solution)/shard_map/reduce_sum | solution.py:44
  353.1 2.7 collective-permute-start.48
  356.9 3.2 collective-permute-start.52
  360.1 1.8 collective-permute-start.55
  371.7 3.2 collective-permute-start.56
  375.0 1.7 collective-permute-done.57
  380.0 3.2 collective-permute-start.60
  383.3 1.7 collective-permute-done.61
  389.8 3.2 collective-permute-start.64
  395.1 12.0 %all_to_all.36 = f32[16,1,1]{2,1,0:T(1,128)S(1)} all-to-all(f32[16,1,1]{2,1,0:T(1,128)S(1)} %broadcast_in_dim.44), channel_id=1, replica_groups=mesh['tx'=8,'ty'=2,'vel'=16] {'tx','ty'}, dimensions={0} | all-to-all | bytes 128 | tf_op jit(solution)/shard_map/all_to_all | solution.py:40
  412.0 2.8 convolution_add_fusion
  417.9 2.9 collective-permute-start.69
  421.4 1.6 collective-permute-done.70
  423.1 4.2 collective-permute-done.71
  427.3 8.5 %multiply_select_fusion = f32[8,8,16,768]{3,2,1,0:T(8,128)} fusion(f32[8,8,16,768]{3,2,1,0:T(8,128)S(1)} %convolution_add_fusion, f32[8,1,16,768]{3,2,1,0:T(8,128)S(1)} %collective-permute-done.71, f32[1,8,16,768]{3,2,1,0:T(8,128)S(1)} %collective-permute-done.69, f32[1,8,16,768]{3,2,1,0:T(8,128)S(1)} %collective-permute-done.68, ...), kind=kOutput, calls=%fused_computation | convolution fusion | flops 78643200 | bytes 14218240 | tf_op jit(solution)/shard_map/kxyz,kv->xyzv/dot_general | solution.py:203
  (433 shorter events, 103.5 us)
Async XLA Ops:
  26.8 23.0 %all-to-all-start = ((f32[16,1,14336]{2,1,0:T(1,128)}), f32[16,1,14336]{2,1,0:T(1,128)S(1)}, u32[]{:S(2)}, u32[]{:S(2)}) async-start(f32[16,1,14336]{2,1,0:T(1,128)} %reshape.53), calls=%async_computation | async-start | bytes 1835008 | tf_op jit(solution)/shard_map/all_to_all | solution.py:40
  61.6 8.2 %collective-permute-start.3 = (f32[5,8,1,16]{3,2,1,0:T(1,128)S(1)}, f32[5,8,1,16]{3,2,1,0:T(1,128)S(1)}, u32[]{:S(2)}, u32[]{:S(2)}) collective-permute-start(f32[5,8,1,16]{3,2,1,0:T(1,128)S(1)} %get-tuple-element.86), channel_id=1, source_target_pairs={{0,16},{16,0},{1,17},{17,1},{2,18},{18,2},{3,19},{19,3},{4,20},{20... | collective-permute-start | bytes 7688 | tf_op jit(solution)/shard_map/ppermute | solution.py:26
  63.0 10.0 %collective-permute-start.2 = (f32[5,8,1,16]{3,2,1,0:T(1,128)S(1)}, f32[5,8,1,16]{3,2,1,0:T(1,128)S(1)}, u32[]{:S(2)}, u32[]{:S(2)}) collective-permute-start(f32[5,8,1,16]{3,2,1,0:T(1,128)S(1)} %get-tuple-element.87), channel_id=1, source_target_pairs={{16,0},{0,16},{17,1},{1,17},{18,2},{2,18},{19,3},{3,19},{20,4},{4,... | collective-permute-start | bytes 7688 | tf_op jit(solution)/shard_map/ppermute | solution.py:27
  63.7 10.8 %collective-permute-start.1 = (f32[5,1,8,16]{3,2,1,0:T(8,128)S(1)}, f32[5,1,8,16]{3,2,1,0:T(8,128)S(1)}, u32[]{:S(2)}, u32[]{:S(2)}) collective-permute-start(f32[5,1,8,16]{3,2,1,0:T(8,128)S(1)} %get-tuple-element.88), channel_id=1, source_target_pairs={{0,32},{32,64},{64,96},{96,128},{128,160},{160,192},{192,224},{224... | collective-permute-start | bytes 7688 | tf_op jit(solution)/shard_map/ppermute | solution.py:26
  65.6 10.2 %collective-permute-start = (f32[5,1,8,16]{3,2,1,0:T(8,128)S(1)}, f32[5,1,8,16]{3,2,1,0:T(8,128)S(1)}, u32[]{:S(2)}, u32[]{:S(2)}) collective-permute-start(f32[5,1,8,16]{3,2,1,0:T(8,128)S(1)} %get-tuple-element.89), channel_id=1, source_target_pairs={{32,0},{64,32},{96,64},{128,96},{160,128},{192,160},{224,192},{0,2... | collective-permute-start | bytes 7688 | tf_op jit(solution)/shard_map/ppermute | solution.py:27
  69.7 9.6 %collective-permute-start.5 = (f32[13,1,8,16]{3,2,1,0:T(8,128)S(1)}, f32[13,1,8,16]{3,2,1,0:T(8,128)S(1)}, u32[]{:S(2)}, u32[]{:S(2)}) collective-permute-start(f32[13,1,8,16]{3,2,1,0:T(8,128)S(1)} %get-tuple-element.100), channel_id=1, source_target_pairs={{0,32},{32,64},{64,96},{96,128},{128,160},{160,192},{192,224},{224... | collective-permute-start | bytes 19976 | tf_op jit(solution)/shard_map/ppermute | solution.py:26
  69.8 9.5 %collective-permute-start.4 = (f32[13,1,8,16]{3,2,1,0:T(8,128)S(1)}, f32[13,1,8,16]{3,2,1,0:T(8,128)S(1)}, u32[]{:S(2)}, u32[]{:S(2)}) collective-permute-start(f32[13,1,8,16]{3,2,1,0:T(8,128)S(1)} %get-tuple-element.101), channel_id=1, source_target_pairs={{32,0},{64,32},{96,64},{128,96},{160,128},{192,160},{224,192},{0,2... | collective-permute-start | bytes 19976 | tf_op jit(solution)/shard_map/ppermute | solution.py:27
  81.7 5.4 %collective-permute-start.11 = (f32[5,8,1,16]{3,2,1,0:T(1,128)S(1)}, f32[5,8,1,16]{3,2,1,0:T(1,128)S(1)}, u32[]{:S(2)}, u32[]{:S(2)}) collective-permute-start(f32[5,8,1,16]{3,2,1,0:T(1,128)S(1)} %get-tuple-element.186), channel_id=1, source_target_pairs={{0,16},{16,0},{1,17},{17,1},{2,18},{18,2},{3,19},{19,3},{4,20},{20... | collective-permute-start | bytes 7688 | tf_op jit(solution)/shard_map/ppermute | solution.py:26
  83.9 5.0 %collective-permute-start.9 = (f32[5,1,8,16]{3,2,1,0:T(8,128)S(1)}, f32[5,1,8,16]{3,2,1,0:T(8,128)S(1)}, u32[]{:S(2)}, u32[]{:S(2)}) collective-permute-start(f32[5,1,8,16]{3,2,1,0:T(8,128)S(1)} %get-tuple-element.188), channel_id=1, source_target_pairs={{0,32},{32,64},{64,96},{96,128},{128,160},{160,192},{192,224},{224... | collective-permute-start | bytes 7688 | tf_op jit(solution)/shard_map/ppermute | solution.py:26
  83.9 5.0 %collective-permute-start.8 = (f32[5,1,8,16]{3,2,1,0:T(8,128)S(1)}, f32[5,1,8,16]{3,2,1,0:T(8,128)S(1)}, u32[]{:S(2)}, u32[]{:S(2)}) collective-permute-start(f32[5,1,8,16]{3,2,1,0:T(8,128)S(1)} %get-tuple-element.189), channel_id=1, source_target_pairs={{32,0},{64,32},{96,64},{128,96},{160,128},{192,160},{224,192},{0,2... | collective-permute-start | bytes 7688 | tf_op jit(solution)/shard_map/ppermute | solution.py:27
  90.0 6.1 %collective-permute-start.15 = (f32[5,8,1,16]{3,2,1,0:T(1,128)S(1)}, f32[5,8,1,16]{3,2,1,0:T(1,128)S(1)}, u32[]{:S(2)}, u32[]{:S(2)}) collective-permute-start(f32[5,8,1,16]{3,2,1,0:T(1,128)S(1)} %get-tuple-element.182), channel_id=1, source_target_pairs={{0,16},{16,0},{1,17},{17,1},{2,18},{18,2},{3,19},{19,3},{4,20},{20... | collective-permute-start | bytes 7688 | tf_op jit(solution)/shard_map/ppermute | solution.py:26
  90.8 5.4 %collective-permute-start.14 = (f32[5,8,1,16]{3,2,1,0:T(1,128)S(1)}, f32[5,8,1,16]{3,2,1,0:T(1,128)S(1)}, u32[]{:S(2)}, u32[]{:S(2)}) collective-permute-start(f32[5,8,1,16]{3,2,1,0:T(1,128)S(1)} %get-tuple-element.183), channel_id=1, source_target_pairs={{16,0},{0,16},{17,1},{1,17},{18,2},{2,18},{19,3},{3,19},{20,4},{4,... | collective-permute-start | bytes 7688 | tf_op jit(solution)/shard_map/ppermute | solution.py:27
  92.1 5.0 %collective-permute-start.13 = (f32[5,1,8,16]{3,2,1,0:T(8,128)S(1)}, f32[5,1,8,16]{3,2,1,0:T(8,128)S(1)}, u32[]{:S(2)}, u32[]{:S(2)}) collective-permute-start(f32[5,1,8,16]{3,2,1,0:T(8,128)S(1)} %get-tuple-element.184), channel_id=1, source_target_pairs={{0,32},{32,64},{64,96},{96,128},{128,160},{160,192},{192,224},{224... | collective-permute-start | bytes 7688 | tf_op jit(solution)/shard_map/ppermute | solution.py:26
  92.1 5.0 %collective-permute-start.12 = (f32[5,1,8,16]{3,2,1,0:T(8,128)S(1)}, f32[5,1,8,16]{3,2,1,0:T(8,128)S(1)}, u32[]{:S(2)}, u32[]{:S(2)}) collective-permute-start(f32[5,1,8,16]{3,2,1,0:T(8,128)S(1)} %get-tuple-element.185), channel_id=1, source_target_pairs={{32,0},{64,32},{96,64},{128,96},{160,128},{192,160},{224,192},{0,2... | collective-permute-start | bytes 7688 | tf_op jit(solution)/shard_map/ppermute | solution.py:27
  98.3 23.3 %collective-permute-start.19 = (f32[5,8,1,16]{3,2,1,0:T(1,128)S(1)}, f32[5,8,1,16]{3,2,1,0:T(1,128)S(1)}, u32[]{:S(2)}, u32[]{:S(2)}) collective-permute-start(f32[5,8,1,16]{3,2,1,0:T(1,128)S(1)} %get-tuple-element.178), channel_id=1, source_target_pairs={{0,16},{16,0},{1,17},{17,1},{2,18},{18,2},{3,19},{19,3},{4,20},{20... | collective-permute-start | bytes 7688 | tf_op jit(solution)/shard_map/ppermute | solution.py:26
  99.1 22.5 %collective-permute-start.18 = (f32[5,8,1,16]{3,2,1,0:T(1,128)S(1)}, f32[5,8,1,16]{3,2,1,0:T(1,128)S(1)}, u32[]{:S(2)}, u32[]{:S(2)}) collective-permute-start(f32[5,8,1,16]{3,2,1,0:T(1,128)S(1)} %get-tuple-element.179), channel_id=1, source_target_pairs={{16,0},{0,16},{17,1},{1,17},{18,2},{2,18},{19,3},{3,19},{20,4},{4,... | collective-permute-start | bytes 7688 | tf_op jit(solution)/shard_map/ppermute | solution.py:27
  100.4 21.2 %collective-permute-start.17 = (f32[5,1,8,16]{3,2,1,0:T(8,128)S(1)}, f32[5,1,8,16]{3,2,1,0:T(8,128)S(1)}, u32[]{:S(2)}, u32[]{:S(2)}) collective-permute-start(f32[5,1,8,16]{3,2,1,0:T(8,128)S(1)} %get-tuple-element.180), channel_id=1, source_target_pairs={{0,32},{32,64},{64,96},{96,128},{128,160},{160,192},{192,224},{224... | collective-permute-start | bytes 7688 | tf_op jit(solution)/shard_map/ppermute | solution.py:26
  103.7 18.0 %collective-permute-start.16 = (f32[5,1,8,16]{3,2,1,0:T(8,128)S(1)}, f32[5,1,8,16]{3,2,1,0:T(8,128)S(1)}, u32[]{:S(2)}, u32[]{:S(2)}) collective-permute-start(f32[5,1,8,16]{3,2,1,0:T(8,128)S(1)} %get-tuple-element.181), channel_id=1, source_target_pairs={{32,0},{64,32},{96,64},{128,96},{160,128},{192,160},{224,192},{0,2... | collective-permute-start | bytes 7688 | tf_op jit(solution)/shard_map/ppermute | solution.py:27
  106.0 14.3 %all-to-all-start.1 = ((f32[16,1,1]{2,1,0:T(1,128)}), f32[16,1,1]{2,1,0:T(1,128)S(1)}, u32[]{:S(2)}, u32[]{:S(2)}) async-start(f32[16,1,1]{2,1,0:T(1,128)} %broadcast_in_dim.40), calls=%async_computation.1 | async-start | bytes 16384 | tf_op jit(solution)/shard_map/all_to_all | solution.py:40
  126.9 7.9 %collective-permute-start.22 = (f32[8,1,16,768]{3,2,1,0:T(8,128)S(1)}, f32[8,1,16,768]{3,2,1,0:T(8,128)S(1)}, u32[]{:S(2)}, u32[]{:S(2)}) collective-permute-start(f32[8,1,16,768]{3,2,1,0:T(8,128)S(1)} %get-tuple-element.62), channel_id=1, source_target_pairs={{0,16},{16,0},{1,17},{17,1},{2,18},{18,2},{3,19},{19,3},{4,20},{20... | collective-permute-start | bytes 1179656 | tf_op jit(solution)/shard_map/ppermute | solution.py:26
  128.4 10.5 %collective-permute-start.23 = (f32[8,1,16,768]{3,2,1,0:T(8,128)S(1)}, f32[8,1,16,768]{3,2,1,0:T(8,128)S(1)}, u32[]{:S(2)}, u32[]{:S(2)}) collective-permute-start(f32[8,1,16,768]{3,2,1,0:T(8,128)S(1)} %get-tuple-element.63), channel_id=1, source_target_pairs={{16,0},{0,16},{17,1},{1,17},{18,2},{2,18},{19,3},{3,19},{20,4},{4,... | collective-permute-start | bytes 1179656 | tf_op jit(solution)/shard_map/ppermute | solution.py:27
  129.0 10.0 %collective-permute-start.20 = (f32[1,8,16,768]{3,2,1,0:T(8,128)S(1)}, f32[1,8,16,768]{3,2,1,0:T(8,128)S(1)}, u32[]{:S(2)}, u32[]{:S(2)}) collective-permute-start(f32[1,8,16,768]{3,2,1,0:T(8,128)S(1)} %get-tuple-element.64), channel_id=1, source_target_pairs={{0,32},{32,64},{64,96},{96,128},{128,160},{160,192},{192,224},{224... | collective-permute-start | bytes 1179656 | tf_op jit(solution)/shard_map/ppermute | solution.py:26
  129.6 9.4 %collective-permute-start.21 = (f32[1,8,16,768]{3,2,1,0:T(8,128)S(1)}, f32[1,8,16,768]{3,2,1,0:T(8,128)S(1)}, u32[]{:S(2)}, u32[]{:S(2)}) collective-permute-start(f32[1,8,16,768]{3,2,1,0:T(8,128)S(1)} %get-tuple-element.65), channel_id=1, source_target_pairs={{32,0},{64,32},{96,64},{128,96},{160,128},{192,160},{224,192},{0,2... | collective-permute-start | bytes 1179656 | tf_op jit(solution)/shard_map/ppermute | solution.py:27
  206.1 6.5 %collective-permute-start.27 = (f32[5,8,1,16]{3,2,1,0:T(1,128)S(1)}, f32[5,8,1,16]{3,2,1,0:T(1,128)S(1)}, u32[]{:S(2)}, u32[]{:S(2)}) collective-permute-start(f32[5,8,1,16]{3,2,1,0:T(1,128)S(1)} %get-tuple-element.82), channel_id=1, source_target_pairs={{0,16},{16,0},{1,17},{17,1},{2,18},{18,2},{3,19},{19,3},{4,20},{20... | collective-permute-start | bytes 7688 | tf_op jit(solution)/shard_map/ppermute | solution.py:26
  207.7 8.2 %collective-permute-start.26 = (f32[5,8,1,16]{3,2,1,0:T(1,128)S(1)}, f32[5,8,1,16]{3,2,1,0:T(1,128)S(1)}, u32[]{:S(2)}, u32[]{:S(2)}) collective-permute-start(f32[5,8,1,16]{3,2,1,0:T(1,128)S(1)} %get-tuple-element.83), channel_id=1, source_target_pairs={{16,0},{0,16},{17,1},{1,17},{18,2},{2,18},{19,3},{3,19},{20,4},{4,... | collective-permute-start | bytes 7688 | tf_op jit(solution)/shard_map/ppermute | solution.py:27
  208.2 9.4 %collective-permute-start.25 = (f32[5,1,8,16]{3,2,1,0:T(8,128)S(1)}, f32[5,1,8,16]{3,2,1,0:T(8,128)S(1)}, u32[]{:S(2)}, u32[]{:S(2)}) collective-permute-start(f32[5,1,8,16]{3,2,1,0:T(8,128)S(1)} %get-tuple-element.84), channel_id=1, source_target_pairs={{0,32},{32,64},{64,96},{96,128},{128,160},{160,192},{192,224},{224... | collective-permute-start | bytes 7688 | tf_op jit(solution)/shard_map/ppermute | solution.py:26
  208.8 9.5 %collective-permute-start.24 = (f32[5,1,8,16]{3,2,1,0:T(8,128)S(1)}, f32[5,1,8,16]{3,2,1,0:T(8,128)S(1)}, u32[]{:S(2)}, u32[]{:S(2)}) collective-permute-start(f32[5,1,8,16]{3,2,1,0:T(8,128)S(1)} %get-tuple-element.85), channel_id=1, source_target_pairs={{32,0},{64,32},{96,64},{128,96},{160,128},{192,160},{224,192},{0,2... | collective-permute-start | bytes 7688 | tf_op jit(solution)/shard_map/ppermute | solution.py:27
  212.5 9.4 %collective-permute-start.29 = (f32[13,1,8,16]{3,2,1,0:T(8,128)S(1)}, f32[13,1,8,16]{3,2,1,0:T(8,128)S(1)}, u32[]{:S(2)}, u32[]{:S(2)}) collective-permute-start(f32[13,1,8,16]{3,2,1,0:T(8,128)S(1)} %get-tuple-element.96), channel_id=1, source_target_pairs={{0,32},{32,64},{64,96},{96,128},{128,160},{160,192},{192,224},{224... | collective-permute-start | bytes 19976 | tf_op jit(solution)/shard_map/ppermute | solution.py:26
  212.6 9.3 %collective-permute-start.28 = (f32[13,1,8,16]{3,2,1,0:T(8,128)S(1)}, f32[13,1,8,16]{3,2,1,0:T(8,128)S(1)}, u32[]{:S(2)}, u32[]{:S(2)}) collective-permute-start(f32[13,1,8,16]{3,2,1,0:T(8,128)S(1)} %get-tuple-element.97), channel_id=1, source_target_pairs={{32,0},{64,32},{96,64},{128,96},{160,128},{192,160},{224,192},{0,2... | collective-permute-start | bytes 19976 | tf_op jit(solution)/shard_map/ppermute | solution.py:27
  225.2 5.4 %collective-permute-start.35 = (f32[5,8,1,16]{3,2,1,0:T(1,128)S(1)}, f32[5,8,1,16]{3,2,1,0:T(1,128)S(1)}, u32[]{:S(2)}, u32[]{:S(2)}) collective-permute-start(f32[5,8,1,16]{3,2,1,0:T(1,128)S(1)} %get-tuple-element.172), channel_id=1, source_target_pairs={{0,16},{16,0},{1,17},{17,1},{2,18},{18,2},{3,19},{19,3},{4,20},{20... | collective-permute-start | bytes 7688 | tf_op jit(solution)/shard_map/ppermute | solution.py:26
  227.3 5.0 %collective-permute-start.33 = (f32[5,1,8,16]{3,2,1,0:T(8,128)S(1)}, f32[5,1,8,16]{3,2,1,0:T(8,128)S(1)}, u32[]{:S(2)}, u32[]{:S(2)}) collective-permute-start(f32[5,1,8,16]{3,2,1,0:T(8,128)S(1)} %get-tuple-element.174), channel_id=1, source_target_pairs={{0,32},{32,64},{64,96},{96,128},{128,160},{160,192},{192,224},{224... | collective-permute-start | bytes 7688 | tf_op jit(solution)/shard_map/ppermute | solution.py:26
  227.3 5.0 %collective-permute-start.32 = (f32[5,1,8,16]{3,2,1,0:T(8,128)S(1)}, f32[5,1,8,16]{3,2,1,0:T(8,128)S(1)}, u32[]{:S(2)}, u32[]{:S(2)}) collective-permute-start(f32[5,1,8,16]{3,2,1,0:T(8,128)S(1)} %get-tuple-element.175), channel_id=1, source_target_pairs={{32,0},{64,32},{96,64},{128,96},{160,128},{192,160},{224,192},{0,2... | collective-permute-start | bytes 7688 | tf_op jit(solution)/shard_map/ppermute | solution.py:27
  233.5 5.4 %collective-permute-start.39 = (f32[5,8,1,16]{3,2,1,0:T(1,128)S(1)}, f32[5,8,1,16]{3,2,1,0:T(1,128)S(1)}, u32[]{:S(2)}, u32[]{:S(2)}) collective-permute-start(f32[5,8,1,16]{3,2,1,0:T(1,128)S(1)} %get-tuple-element.168), channel_id=1, source_target_pairs={{0,16},{16,0},{1,17},{17,1},{2,18},{18,2},{3,19},{19,3},{4,20},{20... | collective-permute-start | bytes 7688 | tf_op jit(solution)/shard_map/ppermute | solution.py:26
  235.6 5.0 %collective-permute-start.37 = (f32[5,1,8,16]{3,2,1,0:T(8,128)S(1)}, f32[5,1,8,16]{3,2,1,0:T(8,128)S(1)}, u32[]{:S(2)}, u32[]{:S(2)}) collective-permute-start(f32[5,1,8,16]{3,2,1,0:T(8,128)S(1)} %get-tuple-element.170), channel_id=1, source_target_pairs={{0,32},{32,64},{64,96},{96,128},{128,160},{160,192},{192,224},{224... | collective-permute-start | bytes 7688 | tf_op jit(solution)/shard_map/ppermute | solution.py:26
  235.6 5.0 %collective-permute-start.36 = (f32[5,1,8,16]{3,2,1,0:T(8,128)S(1)}, f32[5,1,8,16]{3,2,1,0:T(8,128)S(1)}, u32[]{:S(2)}, u32[]{:S(2)}) collective-permute-start(f32[5,1,8,16]{3,2,1,0:T(8,128)S(1)} %get-tuple-element.171), channel_id=1, source_target_pairs={{32,0},{64,32},{96,64},{128,96},{160,128},{192,160},{224,192},{0,2... | collective-permute-start | bytes 7688 | tf_op jit(solution)/shard_map/ppermute | solution.py:27
  243.0 21.7 %collective-permute-start.43 = (f32[5,8,1,16]{3,2,1,0:T(1,128)}, f32[5,8,1,16]{3,2,1,0:T(1,128)}, u32[]{:S(2)}, u32[]{:S(2)}) collective-permute-start(f32[5,8,1,16]{3,2,1,0:T(1,128)} %get-tuple-element.164), channel_id=1, source_target_pairs={{0,16},{16,0},{1,17},{17,1},{2,18},{18,2},{3,19},{19,3},{4,20},{20... | collective-permute-start | bytes 7688 | tf_op jit(solution)/shard_map/ppermute | solution.py:26
  243.7 21.7 %collective-permute-start.42 = (f32[5,8,1,16]{3,2,1,0:T(1,128)}, f32[5,8,1,16]{3,2,1,0:T(1,128)}, u32[]{:S(2)}, u32[]{:S(2)}) collective-permute-start(f32[5,8,1,16]{3,2,1,0:T(1,128)} %get-tuple-element.165), channel_id=1, source_target_pairs={{16,0},{0,16},{17,1},{1,17},{18,2},{2,18},{19,3},{3,19},{20,4},{4,... | collective-permute-start | bytes 7688 | tf_op jit(solution)/shard_map/ppermute | solution.py:27
  245.2 21.0 %collective-permute-start.41 = (f32[5,1,8,16]{3,2,1,0:T(8,128)}, f32[5,1,8,16]{3,2,1,0:T(8,128)S(1)}, u32[]{:S(2)}, u32[]{:S(2)}) collective-permute-start(f32[5,1,8,16]{3,2,1,0:T(8,128)} %get-tuple-element.166), channel_id=1, source_target_pairs={{0,32},{32,64},{64,96},{96,128},{128,160},{160,192},{192,224},{224... | collective-permute-start | bytes 7688 | tf_op jit(solution)/shard_map/ppermute | solution.py:26
  245.2 21.0 %collective-permute-start.40 = (f32[5,1,8,16]{3,2,1,0:T(8,128)}, f32[5,1,8,16]{3,2,1,0:T(8,128)S(1)}, u32[]{:S(2)}, u32[]{:S(2)}) collective-permute-start(f32[5,1,8,16]{3,2,1,0:T(8,128)} %get-tuple-element.167), channel_id=1, source_target_pairs={{32,0},{64,32},{96,64},{128,96},{160,128},{192,160},{224,192},{0,2... | collective-permute-start | bytes 7688 | tf_op jit(solution)/shard_map/ppermute | solution.py:27
  271.5 7.9 %collective-permute-start.46 = (f32[8,1,16,768]{3,2,1,0:T(8,128)S(1)}, f32[8,1,16,768]{3,2,1,0:T(8,128)S(1)}, u32[]{:S(2)}, u32[]{:S(2)}) collective-permute-start(f32[8,1,16,768]{3,2,1,0:T(8,128)S(1)} %get-tuple-element.54), channel_id=1, source_target_pairs={{0,16},{16,0},{1,17},{17,1},{2,18},{18,2},{3,19},{19,3},{4,20},{20... | collective-permute-start | bytes 1179656 | tf_op jit(solution)/shard_map/ppermute | solution.py:26
  273.1 10.5 %collective-permute-start.47 = (f32[8,1,16,768]{3,2,1,0:T(8,128)S(1)}, f32[8,1,16,768]{3,2,1,0:T(8,128)S(1)}, u32[]{:S(2)}, u32[]{:S(2)}) collective-permute-start(f32[8,1,16,768]{3,2,1,0:T(8,128)S(1)} %get-tuple-element.55), channel_id=1, source_target_pairs={{16,0},{0,16},{17,1},{1,17},{18,2},{2,18},{19,3},{3,19},{20,4},{4,... | collective-permute-start | bytes 1179656 | tf_op jit(solution)/shard_map/ppermute | solution.py:27
  273.6 10.0 %collective-permute-start.44 = (f32[1,8,16,768]{3,2,1,0:T(8,128)S(1)}, f32[1,8,16,768]{3,2,1,0:T(8,128)S(1)}, u32[]{:S(2)}, u32[]{:S(2)}) collective-permute-start(f32[1,8,16,768]{3,2,1,0:T(8,128)S(1)} %get-tuple-element.56), channel_id=1, source_target_pairs={{0,32},{32,64},{64,96},{96,128},{128,160},{160,192},{192,224},{224... | collective-permute-start | bytes 1179656 | tf_op jit(solution)/shard_map/ppermute | solution.py:26
  274.2 9.4 %collective-permute-start.45 = (f32[1,8,16,768]{3,2,1,0:T(8,128)S(1)}, f32[1,8,16,768]{3,2,1,0:T(8,128)S(1)}, u32[]{:S(2)}, u32[]{:S(2)}) collective-permute-start(f32[1,8,16,768]{3,2,1,0:T(8,128)S(1)} %get-tuple-element.57), channel_id=1, source_target_pairs={{32,0},{64,32},{96,64},{128,96},{160,128},{192,160},{224,192},{0,2... | collective-permute-start | bytes 1179656 | tf_op jit(solution)/shard_map/ppermute | solution.py:27
  350.4 6.5 %collective-permute-start.51 = (f32[5,8,1,16]{3,2,1,0:T(1,128)S(1)}, f32[5,8,1,16]{3,2,1,0:T(1,128)S(1)}, u32[]{:S(2)}, u32[]{:S(2)}) collective-permute-start(f32[5,8,1,16]{3,2,1,0:T(1,128)S(1)} %get-tuple-element.78), channel_id=1, source_target_pairs={{0,16},{16,0},{1,17},{17,1},{2,18},{18,2},{3,19},{19,3},{4,20},{20... | collective-permute-start | bytes 7688 | tf_op jit(solution)/shard_map/ppermute | solution.py:26
  352.0 8.2 %collective-permute-start.50 = (f32[5,8,1,16]{3,2,1,0:T(1,128)S(1)}, f32[5,8,1,16]{3,2,1,0:T(1,128)S(1)}, u32[]{:S(2)}, u32[]{:S(2)}) collective-permute-start(f32[5,8,1,16]{3,2,1,0:T(1,128)S(1)} %get-tuple-element.79), channel_id=1, source_target_pairs={{16,0},{0,16},{17,1},{1,17},{18,2},{2,18},{19,3},{3,19},{20,4},{4,... | collective-permute-start | bytes 7688 | tf_op jit(solution)/shard_map/ppermute | solution.py:27
  352.5 9.4 %collective-permute-start.49 = (f32[5,1,8,16]{3,2,1,0:T(8,128)S(1)}, f32[5,1,8,16]{3,2,1,0:T(8,128)S(1)}, u32[]{:S(2)}, u32[]{:S(2)}) collective-permute-start(f32[5,1,8,16]{3,2,1,0:T(8,128)S(1)} %get-tuple-element.80), channel_id=1, source_target_pairs={{0,32},{32,64},{64,96},{96,128},{128,160},{160,192},{192,224},{224... | collective-permute-start | bytes 7688 | tf_op jit(solution)/shard_map/ppermute | solution.py:26
  353.1 9.5 %collective-permute-start.48 = (f32[5,1,8,16]{3,2,1,0:T(8,128)S(1)}, f32[5,1,8,16]{3,2,1,0:T(8,128)S(1)}, u32[]{:S(2)}, u32[]{:S(2)}) collective-permute-start(f32[5,1,8,16]{3,2,1,0:T(8,128)S(1)} %get-tuple-element.81), channel_id=1, source_target_pairs={{32,0},{64,32},{96,64},{128,96},{160,128},{192,160},{224,192},{0,2... | collective-permute-start | bytes 7688 | tf_op jit(solution)/shard_map/ppermute | solution.py:27
  356.8 9.4 %collective-permute-start.53 = (f32[13,1,8,16]{3,2,1,0:T(8,128)S(1)}, f32[13,1,8,16]{3,2,1,0:T(8,128)S(1)}, u32[]{:S(2)}, u32[]{:S(2)}) collective-permute-start(f32[13,1,8,16]{3,2,1,0:T(8,128)S(1)} %get-tuple-element.92), channel_id=1, source_target_pairs={{0,32},{32,64},{64,96},{96,128},{128,160},{160,192},{192,224},{224... | collective-permute-start | bytes 19976 | tf_op jit(solution)/shard_map/ppermute | solution.py:26
  356.9 9.3 %collective-permute-start.52 = (f32[13,1,8,16]{3,2,1,0:T(8,128)S(1)}, f32[13,1,8,16]{3,2,1,0:T(8,128)S(1)}, u32[]{:S(2)}, u32[]{:S(2)}) collective-permute-start(f32[13,1,8,16]{3,2,1,0:T(8,128)S(1)} %get-tuple-element.93), channel_id=1, source_target_pairs={{32,0},{64,32},{96,64},{128,96},{160,128},{192,160},{224,192},{0,2... | collective-permute-start | bytes 19976 | tf_op jit(solution)/shard_map/ppermute | solution.py:27
  369.6 5.4 %collective-permute-start.59 = (f32[5,8,1,16]{3,2,1,0:T(1,128)S(1)}, f32[5,8,1,16]{3,2,1,0:T(1,128)S(1)}, u32[]{:S(2)}, u32[]{:S(2)}) collective-permute-start(f32[5,8,1,16]{3,2,1,0:T(1,128)S(1)} %get-tuple-element.158), channel_id=1, source_target_pairs={{0,16},{16,0},{1,17},{17,1},{2,18},{18,2},{3,19},{19,3},{4,20},{20... | collective-permute-start | bytes 7688 | tf_op jit(solution)/shard_map/ppermute | solution.py:26
  370.2 4.8 %collective-permute-start.58 = (f32[5,8,1,16]{3,2,1,0:T(1,128)S(1)}, f32[5,8,1,16]{3,2,1,0:T(1,128)S(1)}, u32[]{:S(2)}, u32[]{:S(2)}) collective-permute-start(f32[5,8,1,16]{3,2,1,0:T(1,128)S(1)} %get-tuple-element.159), channel_id=1, source_target_pairs={{16,0},{0,16},{17,1},{1,17},{18,2},{2,18},{19,3},{3,19},{20,4},{4,... | collective-permute-start | bytes 7688 | tf_op jit(solution)/shard_map/ppermute | solution.py:27
  371.7 5.0 %collective-permute-start.57 = (f32[5,1,8,16]{3,2,1,0:T(8,128)S(1)}, f32[5,1,8,16]{3,2,1,0:T(8,128)S(1)}, u32[]{:S(2)}, u32[]{:S(2)}) collective-permute-start(f32[5,1,8,16]{3,2,1,0:T(8,128)S(1)} %get-tuple-element.160), channel_id=1, source_target_pairs={{0,32},{32,64},{64,96},{96,128},{128,160},{160,192},{192,224},{224... | collective-permute-start | bytes 7688 | tf_op jit(solution)/shard_map/ppermute | solution.py:26
  371.7 5.0 %collective-permute-start.56 = (f32[5,1,8,16]{3,2,1,0:T(8,128)S(1)}, f32[5,1,8,16]{3,2,1,0:T(8,128)S(1)}, u32[]{:S(2)}, u32[]{:S(2)}) collective-permute-start(f32[5,1,8,16]{3,2,1,0:T(8,128)S(1)} %get-tuple-element.161), channel_id=1, source_target_pairs={{32,0},{64,32},{96,64},{128,96},{160,128},{192,160},{224,192},{0,2... | collective-permute-start | bytes 7688 | tf_op jit(solution)/shard_map/ppermute | solution.py:27
  377.9 5.4 %collective-permute-start.63 = (f32[5,8,1,16]{3,2,1,0:T(1,128)S(1)}, f32[5,8,1,16]{3,2,1,0:T(1,128)S(1)}, u32[]{:S(2)}, u32[]{:S(2)}) collective-permute-start(f32[5,8,1,16]{3,2,1,0:T(1,128)S(1)} %get-tuple-element.154), channel_id=1, source_target_pairs={{0,16},{16,0},{1,17},{17,1},{2,18},{18,2},{3,19},{19,3},{4,20},{20... | collective-permute-start | bytes 7688 | tf_op jit(solution)/shard_map/ppermute | solution.py:26
  380.0 5.0 %collective-permute-start.61 = (f32[5,1,8,16]{3,2,1,0:T(8,128)S(1)}, f32[5,1,8,16]{3,2,1,0:T(8,128)S(1)}, u32[]{:S(2)}, u32[]{:S(2)}) collective-permute-start(f32[5,1,8,16]{3,2,1,0:T(8,128)S(1)} %get-tuple-element.156), channel_id=1, source_target_pairs={{0,32},{32,64},{64,96},{96,128},{128,160},{160,192},{192,224},{224... | collective-permute-start | bytes 7688 | tf_op jit(solution)/shard_map/ppermute | solution.py:26
  380.0 5.0 %collective-permute-start.60 = (f32[5,1,8,16]{3,2,1,0:T(8,128)S(1)}, f32[5,1,8,16]{3,2,1,0:T(8,128)S(1)}, u32[]{:S(2)}, u32[]{:S(2)}) collective-permute-start(f32[5,1,8,16]{3,2,1,0:T(8,128)S(1)} %get-tuple-element.157), channel_id=1, source_target_pairs={{32,0},{64,32},{96,64},{128,96},{160,128},{192,160},{224,192},{0,2... | collective-permute-start | bytes 7688 | tf_op jit(solution)/shard_map/ppermute | solution.py:27
  387.3 21.0 %collective-permute-start.67 = (f32[5,8,1,16]{3,2,1,0:T(1,128)}, f32[5,8,1,16]{3,2,1,0:T(1,128)}, u32[]{:S(2)}, u32[]{:S(2)}) collective-permute-start(f32[5,8,1,16]{3,2,1,0:T(1,128)} %get-tuple-element.150), channel_id=1, source_target_pairs={{0,16},{16,0},{1,17},{17,1},{2,18},{18,2},{3,19},{19,3},{4,20},{20... | collective-permute-start | bytes 7688 | tf_op jit(solution)/shard_map/ppermute | solution.py:26
  388.3 20.8 %collective-permute-start.66 = (f32[5,8,1,16]{3,2,1,0:T(1,128)}, f32[5,8,1,16]{3,2,1,0:T(1,128)}, u32[]{:S(2)}, u32[]{:S(2)}) collective-permute-start(f32[5,8,1,16]{3,2,1,0:T(1,128)} %get-tuple-element.151), channel_id=1, source_target_pairs={{16,0},{0,16},{17,1},{1,17},{18,2},{2,18},{19,3},{3,19},{20,4},{4,... | collective-permute-start | bytes 7688 | tf_op jit(solution)/shard_map/ppermute | solution.py:27
  389.7 20.1 %collective-permute-start.65 = (f32[5,1,8,16]{3,2,1,0:T(8,128)}, f32[5,1,8,16]{3,2,1,0:T(8,128)S(1)}, u32[]{:S(2)}, u32[]{:S(2)}) collective-permute-start(f32[5,1,8,16]{3,2,1,0:T(8,128)} %get-tuple-element.152), channel_id=1, source_target_pairs={{0,32},{32,64},{64,96},{96,128},{128,160},{160,192},{192,224},{224... | collective-permute-start | bytes 7688 | tf_op jit(solution)/shard_map/ppermute | solution.py:26
  389.8 20.1 %collective-permute-start.64 = (f32[5,1,8,16]{3,2,1,0:T(8,128)S(1)}, f32[5,1,8,16]{3,2,1,0:T(8,128)S(1)}, u32[]{:S(2)}, u32[]{:S(2)}) collective-permute-start(f32[5,1,8,16]{3,2,1,0:T(8,128)S(1)} %get-tuple-element.153), channel_id=1, source_target_pairs={{32,0},{64,32},{96,64},{128,96},{160,128},{192,160},{224,192},{0,2... | collective-permute-start | bytes 7688 | tf_op jit(solution)/shard_map/ppermute | solution.py:27
  415.2 7.9 %collective-permute-start.70 = (f32[8,1,16,768]{3,2,1,0:T(8,128)S(1)}, f32[8,1,16,768]{3,2,1,0:T(8,128)S(1)}, u32[]{:S(2)}, u32[]{:S(2)}) collective-permute-start(f32[8,1,16,768]{3,2,1,0:T(8,128)S(1)} %get-tuple-element.46), channel_id=1, source_target_pairs={{0,16},{16,0},{1,17},{17,1},{2,18},{18,2},{3,19},{19,3},{4,20},{20... | collective-permute-start | bytes 1179656 | tf_op jit(solution)/shard_map/ppermute | solution.py:26
  416.7 10.5 %collective-permute-start.71 = (f32[8,1,16,768]{3,2,1,0:T(8,128)S(1)}, f32[8,1,16,768]{3,2,1,0:T(8,128)S(1)}, u32[]{:S(2)}, u32[]{:S(2)}) collective-permute-start(f32[8,1,16,768]{3,2,1,0:T(8,128)S(1)} %get-tuple-element.47), channel_id=1, source_target_pairs={{16,0},{0,16},{17,1},{1,17},{18,2},{2,18},{19,3},{3,19},{20,4},{4,... | collective-permute-start | bytes 1179656 | tf_op jit(solution)/shard_map/ppermute | solution.py:27
  417.3 10.0 %collective-permute-start.68 = (f32[1,8,16,768]{3,2,1,0:T(8,128)S(1)}, f32[1,8,16,768]{3,2,1,0:T(8,128)S(1)}, u32[]{:S(2)}, u32[]{:S(2)}) collective-permute-start(f32[1,8,16,768]{3,2,1,0:T(8,128)S(1)} %get-tuple-element.48), channel_id=1, source_target_pairs={{0,32},{32,64},{64,96},{96,128},{128,160},{160,192},{192,224},{224... | collective-permute-start | bytes 1179656 | tf_op jit(solution)/shard_map/ppermute | solution.py:26
  417.9 9.4 %collective-permute-start.69 = (f32[1,8,16,768]{3,2,1,0:T(8,128)S(1)}, f32[1,8,16,768]{3,2,1,0:T(8,128)S(1)}, u32[]{:S(2)}, u32[]{:S(2)}) collective-permute-start(f32[1,8,16,768]{3,2,1,0:T(8,128)S(1)} %get-tuple-element.49), channel_id=1, source_target_pairs={{32,0},{64,32},{96,64},{128,96},{160,128},{192,160},{224,192},{0,2... | collective-permute-start | bytes 1179656 | tf_op jit(solution)/shard_map/ppermute | solution.py:27
  (41 other events, 895.3 us)
where the time goes:
time: 445 us; the launch traced here: 436 us
  starting transfers between devices  116 us (26%)
  local copies, waits for them, and re-layouts  71.9 us (16%)
  blocking collectives  65.3 us (15%)
  matrix products  64.8 us (15%)
  waiting for transfers between devices  57.9 us (13%)
  other arithmetic  54.8 us (12%)
  between operations  5.58 us (1%)
    ppermute x36, starting transfers between devices, extended(): lax.ppermute(first, axis, [(b, a) for a, b in up])  73.1 us
    all_to_all x4, blocking collectives, from_everyone(): return lax.all_to_all(copies, axis, split_axis=0, concat_axis=0, tiled=True)  65.3 us
    dot_general x3, matrix products, on_device(): jnp.einsum('kv,xyzv->kxyz', moment_rows, distribution, precision=highest)  35.6 us
    unnamed x68, local copies, waits for them, and re-layouts  33.8 us
    ppermute x36, starting transfers between devices, extended(): lax.ppermute(last, axis, up)  28.9 us
    all_to_all x2, waiting for transfers between devices, from_everyone(): return lax.all_to_all(copies, axis, split_axis=0, concat_axis=0, tiled=True)  23.6 us
    dot_general x3, matrix products, on_device(): jnp.einsum('kxyz,kv->xyzv', macro_state, rows, precision=highest)  20.7 us
    ppermute x36, waiting for transfers between devices, extended(): lax.ppermute(first, axis, [(b, a) for a, b in up])  17.7 us
  transfers between devices with their start and end apart: 74, of which 20 were waited for; matrix products, arithmetic and copies ran while one was open for 4% of the time, Pallas kernels for 0%

commit v1 on v0

v1 whole, which is shorter than its diff:
```python
import functools

import jax
import jax.numpy as jnp
from jax import lax
from jax.experimental import pallas as pl
from jax.experimental.pallas import tpu as pltpu
from jax.sharding import PartitionSpec as P

ITERS = 3
MACRO_STEPS = 4
NCOMP = 14
MASS = 14
STEP = 0.1
f32 = jnp.float32
bf16 = jnp.bfloat16
MESH = pl.DeviceIdType.MESH
NX, NY, NZ, NV = 8, 8, 16, 768
CELLS = NY * NZ
ROWS = 48
COEF = 40
NEIGHBOURS = [(0, -1), (0, 1), (1, -1), (1, 0), (1, 1)]


def nt(a, b, precision=None):
    return lax.dot_general(a, b, (((1,), (1,)), ((), ())), precision=precision, preferred_element_type=f32)


def tn(a, b):
    return lax.dot_general(a, b, (((0,), (0,)), ((), ())), preferred_element_type=f32)


def rounded(value):
    return value.astype(bf16).astype(f32)


def lanes_of(value):
    return lax.broadcasted_iota(jnp.int32, value.shape, 1)


def other_half(value):
    parts = value.reshape(-1, 2, ROWS // 2, CELLS)
    return jnp.concatenate([parts[:, 1:2], parts[:, 0:1]], axis=1).reshape(value.shape)


def x_next(v):
    return pltpu.roll(v, v.shape[0] - 1, 0)


def x_last(v):
    return pltpu.roll(v, 1, 0)


def y_next(v):
    r = pltpu.roll(v, CELLS - NZ, 1)
    return jnp.where(lanes_of(v) < CELLS - NZ, r, other_half(r))


def y_last(v):
    r = pltpu.roll(v, NZ, 1)
    return jnp.where(lanes_of(v) >= NZ, r, other_half(r))


def z_next(v):
    z = lax.rem(lanes_of(v), NZ)
    return jnp.where(z == NZ - 1, pltpu.roll(v, NZ - 1, 1), pltpu.roll(v, CELLS - 1, 1))


def z_last(v):
    z = lax.rem(lanes_of(v), NZ)
    return jnp.where(z == 0, pltpu.roll(v, CELLS - NZ + 1, 1), pltpu.roll(v, 1, 1))


def field(v, k):
    return v[k * ROWS : (k + 1) * ROWS]


def kernel(
    sizes,
    init_ref, vel_ref, weight_ref, wall_ref, wall_temp_ref, target_ref,
    dist_ref, macro_ref,
    h, stream, edge_y, part, stream_part, rs, near, gathered, tile_mass, mass,
    coef, coef3, rows_f, rows3, proj_f, proj2, mixed3, factors, open_cells, wall_rows, state, source,
    load_sem, rs_send, rs_recv, near_send, near_recv, all_send, all_recv,
    tile_send, tile_recv, mass_send, mass_recv, edge_send, edge_recv,
):
    n_tx, n_ty, n_vel = sizes
    tx, ty, me = lax.axis_index("tx"), lax.axis_index("ty"), lax.axis_index("vel")

    def device(dx, dy, vel):
        return {"tx": lax.rem(tx + (dx + n_tx), n_tx), "ty": lax.rem(ty + dy, n_ty), "vel": vel}

    def group(step):
        return lax.rem(me + step, n_vel)

    far_tiles = [(a, b) for b in range(n_ty) for a in range(n_tx) if (a, b) != (0, 0)]
    near_tiles = [(dx % n_tx, dy) for dy, dx in NEIGHBOURS]
    only_far = [t for t in far_tiles if t not in near_tiles]

    load = pltpu.make_async_copy(init_ref, h.at[0, 0:NX, 0:NY], load_sem)
    load.start()

    barrier = pltpu.get_barrier_semaphore()
    for step in range(1, n_vel):
        pl.semaphore_signal(barrier, inc=1, device_id=device(0, 0, group(step)), device_id_type=MESH)
    for a, b in near_tiles:
        pl.semaphore_signal(barrier, inc=1, device_id=device(a, b, me), device_id_type=MESH)

    @pl.when(me == MASS)
    def _():
        for a, b in only_far:
            pl.semaphore_signal(barrier, inc=1, device_id=device(a, b, me), device_id_type=MESH)

    vx, vy, vz = vel_ref[0:1, :], vel_ref[1:2, :], vel_ref[2:3, :]
    speed_sq = vx * vx + vy * vy + vz * vz
    ones = jnp.ones_like(vx)
    basis = [ones, 2.0 * vx, 2.0 * vy, 2.0 * vz, speed_sq - 1.5]
    sides = []
    for v in (vx, vy, vz):
        sides += [STEP * jnp.maximum(v, 0.0), -STEP * jnp.minimum(v, 0.0)]
    rows = basis + [side * b for side in sides for b in basis] + [basis[4]]
    for copy in range(3):
        for at, row in enumerate(rows):
            rows_f[copy * COEF + at : copy * COEF + at + 1, :] = row
        rows_f[copy * COEF + len(rows) : (copy + 1) * COEF, :] = jnp.zeros((COEF - len(rows), NV), f32)
    rows_f[3 * COEF :, :] = jnp.zeros((128 - 3 * COEF, NV), f32)
    scale = weight_ref[0:1, :] / float(NV * n_vel)
    moments = [ones, vx, vy, vz, (2.0 / 3.0) * speed_sq - 1.0,
               2.0 * (vx * vx - speed_sq / 3.0), 2.0 * (vy * vy - speed_sq / 3.0), 2.0 * (vz * vz - speed_sq / 3.0),
               2.0 * vx * vy, 2.0 * vx * vz, 2.0 * vy * vz,
               vx * (speed_sq - 2.5), vy * (speed_sq - 2.5), vz * (speed_sq - 2.5), ones]
    for at, row in enumerate(moments):
        proj_f[at : at + 1, :] = row * scale
    proj_f[15:16, :] = jnp.zeros((1, NV), f32)
    bx, by, bz = (STEP * jnp.abs(v) for v in (vx, vy, vz))
    for at, row in enumerate((0.9 - bx - by - bz, bx, by, bz, vz)):
        factors[at : at + 1, :] = row
    every = rows_f[...]
    high = rounded(every)
    rows3[...] = jnp.where(lax.broadcasted_iota(jnp.int32, every.shape, 0) < 2 * COEF, high, every - high).astype(bf16)
    proj = proj_f[...]
    proj2[...] = jnp.concatenate([rounded(proj), proj - rounded(proj)], axis=0).astype(bf16)
    mixed = nt(proj, every, lax.Precision.HIGHEST)
    mixed_high = rounded(mixed)
    mixed3[...] = jnp.where(lanes_of(mixed) < 2 * COEF, mixed_high, mixed - mixed_high).astype(bf16)

    solid = jnp.zeros((NX, CELLS), f32)
    heat = jnp.zeros((NX, CELLS), f32)
    for y in range(NY):
        spread = (lax.broadcasted_iota(jnp.int32, (NZ, CELLS), 1)
                  == lax.broadcasted_iota(jnp.int32, (NZ, CELLS), 0) + y * NZ).astype(f32)
        is_wall = (wall_ref[:, y, :] == 1).astype(f32)
        solid = solid + lax.dot_general(is_wall, spread, (((1,), (0,)), ((), ())), precision=lax.Precision.HIGHEST,
                                        preferred_element_type=f32)
        heat = heat + lax.dot_general(is_wall * wall_temp_ref[:, y, :], spread, (((1,), (0,)), ((), ())),
                                      precision=lax.Precision.HIGHEST, preferred_element_type=f32)
    fluid = 1.0 - solid
    wall_rows[0] = fluid
    for x in range(NX):
        open_cells[x] = jnp.broadcast_to(fluid[x : x + 1], (CELLS, CELLS)).T
    coef[35 * NX : 36 * NX, :] = heat
    coef[36 * NX :, :] = jnp.zeros((4 * NX, CELLS), f32)

    def projected(value):
        top = value.astype(bf16)
        low = (value - top.astype(f32)).astype(bf16)
        both = nt(proj2[...], top)
        return both[0:16] + both[16:32] + nt(proj2[0:16, :], low)

    def plane(it, x):
        return h[it, x, 0:NY].reshape(CELLS, NV)

    def pack_edges(it):
        def body(x, _):
            top, bottom = h[it, x, NY - 1], h[it, x, 0]
            for t in range(6):
                cut = slice(t * 128, (t + 1) * 128)
                if t in (0, 3):
                    piece = top[:, cut]
                elif t in (2, 5):
                    piece = bottom[:, cut]
                else:
                    piece = jnp.where(lanes_of(top[:, cut]) < 64, top[:, cut], bottom[:, cut])
                edge_y[it, x, :, cut] = piece
            return 0

        lax.fori_loop(0, NX, body, 0)

    def edge_copies(it):
        half = NV // 2
        return [
            pltpu.make_async_remote_copy(
                src_ref=edge_y.at[it], dst_ref=h.at[it, 0:NX, NY],
                send_sem=edge_send.at[it, 0], recv_sem=edge_recv.at[it, 0],
                device_id=device(0, 1, me), device_id_type=MESH),
            pltpu.make_async_remote_copy(
                src_ref=h.at[it, NX - 1, 0:NY, :, 0:half], dst_ref=h.at[it, NX, 0:NY, :, 0:half],
                send_sem=edge_send.at[it, 1], recv_sem=edge_recv.at[it, 1],
                device_id=device(1, 0, me), device_id_type=MESH),
            pltpu.make_async_remote_copy(
                src_ref=h.at[it, 0, 0:NY, :, half:NV], dst_ref=h.at[it, NX, 0:NY, :, half:NV],
                send_sem=edge_send.at[it, 2], recv_sem=edge_recv.at[it, 2],
                device_id=device(-1, 0, me), device_id_type=MESH),
        ]

    def stream_cell(it, x, y):
        half = NV // 2
        x_down, x_up = lax.rem(x + NX, NX + 1), x + 1
        y_down, y_up = (y + NY) % (NY + 1), y + 1
        for t in range(6):
            cut = slice(t * 128, (t + 1) * 128)
            own = h[it, x, y, :, cut]
            from_x = h[it, x_down if t < 3 else x_up, y, :, cut]
            if t in (0, 3):
                from_y = h[it, x, y_down, :, cut]
            elif t in (2, 5):
                from_y = h[it, x, y_up, :, cut]
            else:
                from_y = jnp.where(lanes_of(own) < 64, h[it, x, y_down, :, cut], h[it, x, y_up, :, cut])
            up = jnp.broadcast_to(factors[4:5, cut], own.shape) > 0.0
            from_z = jnp.where(up, pltpu.roll(own, 1, 0), pltpu.roll(own, NZ - 1, 0))
            value = (factors[0:1, cut] * own + factors[1:2, cut] * from_x
                     + factors[2:3, cut] * from_y + factors[3:4, cut] * from_z)
            stream[x, y, :, cut] = value * open_cells[x, y * NZ : (y + 1) * NZ, :]

    def stream_inside(it):
        def body(x, _):
            for y in range(1, NY - 1):
                stream_cell(it, x, y)
            return 0

        lax.fori_loop(1, NX - 1, body, 0)

    def stream_edges(it):
        def body(x, _):
            stream_cell(it, x, 0)
            stream_cell(it, x, NY - 1)
            return 0

        lax.fori_loop(0, NX, body, 0)

        def ends(side, _):
            for y in range(1, NY - 1):
                stream_cell(it, side * (NX - 1), y)
            return 0

        lax.fori_loop(0, 2, ends, 0)

    def rs_copy(it, step):
        target = group(step)
        return target, pltpu.make_async_remote_copy(
            src_ref=part.at[pl.ds(pl.multiple_of(target * NX, NX), NX)], dst_ref=rs.at[it, step - 1],
            send_sem=rs_send.at[it, step - 1], recv_sem=rs_recv.at[it, step - 1],
            device_id=device(0, 0, target), device_id_type=MESH)

    def near_copies(it):
        return [
            pltpu.make_async_remote_copy(
                src_ref=near.at[it, 1], dst_ref=near.at[it, dy * 3 + 1 - dx],
                send_sem=near_send.at[it, at], recv_sem=near_recv.at[it, dy * 3 + 1 - dx],
                device_id=device(dx, dy, me), device_id_type=MESH)
            for at, (dy, dx) in enumerate(NEIGHBOURS)
        ]

    def all_copy(it, step):
        return pltpu.make_async_remote_copy(
            src_ref=near.at[it], dst_ref=gathered.at[it, me],
            send_sem=all_send.at[it, step - 1], recv_sem=all_recv.at[it, me],
            device_id=device(0, 0, group(step)), device_id_type=MESH)

    def tile_copies(it):
        return [
            pltpu.make_async_remote_copy(
                src_ref=near.at[it, 1], dst_ref=tile_mass.at[it, at],
                send_sem=tile_send.at[it, at], recv_sem=tile_recv.at[it, at],
                device_id=device(a, b, me), device_id_type=MESH)
            for at, (a, b) in enumerate(far_tiles)
        ]

    def mass_copy(it, step):
        return pltpu.make_async_remote_copy(
            src_ref=mass.at[it], dst_ref=mass.at[it],
            send_sem=mass_send.at[it, step - 1], recv_sem=mass_recv.at[it],
            device_id=device(0, 0, group(step)), device_id_type=MESH)

    def macro_solve(it):
        def g(c):
            return gathered[it, c].reshape(ROWS, CELLS)

        def many(*cs):
            return jnp.concatenate([g(c) for c in cs], axis=0)

        flow = many(1, 2, 3, 4)
        along = (many(5, 8, 9, 11), many(8, 6, 10, 12), many(9, 10, 7, 13))
        shifts = ((x_next, x_last), (y_next, y_last), (z_next, z_last))
        total = -6.0 * flow
        for (after, before), a in zip(shifts, along):
            total = total + (after(flow + 0.5 * a) + before(flow - 0.5 * a))
        source[0 : 3 * ROWS] = -0.5 * total[0 : 3 * ROWS]
        source[3 * ROWS :] = -(2.0 / 3.0) * total[3 * ROWS :]
        state[...] = many(0, 1, 2, 3, 4)

        def sweep(_, carry):
            rho, flow = state[0:ROWS], state[ROWS : 5 * ROWS]
            stack = jnp.concatenate([rho + field(flow, 3), flow], axis=0)
            laplace = -6.0 * flow
            grads, divergence = [], None
            for d, (after, before) in enumerate(shifts):
                up, down = after(stack), before(stack)
                laplace = laplace + (up[ROWS:] + down[ROWS:])
                grads.append(0.5 * (field(up, 0) - field(down, 0)))
                part_div = 0.5 * (field(up, 1 + d) - field(down, 1 + d))
                divergence = part_div if divergence is None else divergence + part_div
            state[0:ROWS] = rho - STEP * divergence
            for d in range(3):
                state[(1 + d) * ROWS : (2 + d) * ROWS] = field(flow, d) + STEP * (
                    -0.5 * grads[d] + 0.5 * field(laplace, d) + source[d * ROWS : (d + 1) * ROWS])
            state[4 * ROWS :] = field(flow, 3) + STEP * (
                -(2.0 / 3.0) * divergence + (2.0 / 3.0) * field(laplace, 3) + source[3 * ROWS :])
            return carry

        lax.fori_loop(0, MACRO_STEPS, sweep, 0)

    def coefficients(it):
        shift = target_ref[0, 0] - jnp.sum(mass[it]) / float(NX * NY * NZ * n_tx * n_ty)
        state[0:ROWS] = state[0:ROWS] + shift
        now = state[...]
        was = jnp.concatenate([gathered[it, c].reshape(ROWS, CELLS) for c in range(5)], axis=0)
        change = now - was
        fluid = wall_rows[0]

        def own(value):
            return value.reshape(5, 2, ROWS // 2, CELLS)[:, 0, NX : 2 * NX]

        def put(at, value):
            coef[at * 5 * NX : (at + 1) * 5 * NX, :] = (value * fluid[None]).reshape(5 * NX, CELLS)

        here = own(change)
        put(0, 0.9 * here + STEP * own(now))
        for at, shift_of in enumerate((x_last, x_next, y_last, y_next, z_last, z_next)):
            put(1 + at, own(shift_of(change)) - here)
        for x in range(NX):
            c = coef[pl.ds(x, COEF, stride=NX), :]
            c_high = rounded(c)
            coef3[x] = jnp.concatenate([c_high, c - c_high, c_high, jnp.zeros((8, CELLS), f32)], axis=0).astype(bf16)

    for it in range(ITERS):
        if it == 0:
            load.wait()
            for x in range(NX):
                part[pl.ds(x, 16, stride=NX), :] = projected(plane(0, x))
            greeted = n_vel - 1 + len(near_tiles)

            @pl.when(me == MASS)
            def _():
                pl.semaphore_wait(barrier, greeted + len(only_far))

            @pl.when(me != MASS)
            def _():
                pl.semaphore_wait(barrier, greeted)

        for step in range(1, n_vel):
            target, copy = rs_copy(it, step)
            pl.when(target <= MASS)(copy.start)

        if it > 0:
            def finalize(x, _, it=it):
                new = stream[x].reshape(CELLS, NV) + tn(coef3[x], rows3[...])
                h[it, x, 0:NY] = new.reshape(NY, NZ, NV)
                return 0

            lax.fori_loop(0, NX, finalize, 0)
        pack_edges(it)
        edges = edge_copies(it)
        for copy in edges:
            copy.start()

        @pl.when(me <= MASS)
        def _(it=it):
            total = part[pl.ds(pl.multiple_of(me * NX, NX), NX), :]
            for step in range(1, n_vel):
                rs_copy(it, step)[1].wait_recv()
            for step in range(1, n_vel):
                total = total + rs[it, step - 1]
            near[it, 1] = total

        @pl.when(me < NCOMP)
        def _(it=it):
            for copy in near_copies(it):
                copy.start()

        @pl.when(me == MASS)
        def _(it=it):
            for copy in tile_copies(it):
                copy.start()

        stream_inside(it)

        @pl.when(me < NCOMP)
        def _(it=it):
            for copy in near_copies(it):
                copy.wait_recv()
            for step in range(1, n_vel):
                all_copy(it, step).start()
            gathered[it, me] = near[it]

        @pl.when(me == MASS)
        def _(it=it):
            total = near[it, 1]
            for at, copy in enumerate(tile_copies(it)):
                copy.wait_recv()
                total = total + tile_mass[it, at]
            mass[it] = total
            for step in range(1, n_vel):
                mass_copy(it, step).start()

        for copy in edges:
            copy.wait_recv()
        stream_edges(it)
        if it + 1 < ITERS:
            for x in range(NX):
                stream_part[pl.ds(x, 16, stride=NX), :] = projected(stream[x].reshape(CELLS, NV))

        for c in range(NCOMP):
            @pl.when(me != c)
            def _(it=it, c=c):
                pltpu.make_async_remote_copy(
                    src_ref=near.at[it], dst_ref=gathered.at[it, c],
                    send_sem=all_send.at[it, 0], recv_sem=all_recv.at[it, c],
                    device_id=device(0, 0, group(1)), device_id_type=MESH).wait_recv()

        @pl.when(me != MASS)
        def _(it=it):
            mass_copy(it, 1).wait_recv()

        macro_solve(it)
        coefficients(it)

        for step in range(1, n_vel):
            target, copy = rs_copy(it, step)
            pl.when(target <= MASS)(copy.wait_send)
        if it + 1 < ITERS:
            for x in range(NX):
                at = pl.ds(x, 16, stride=NX)
                part[at, :] = stream_part[at, :] + jnp.dot(mixed3[...], coef3[x], preferred_element_type=f32)

    for x in range(NX):
        new = stream[x].reshape(CELLS, NV) + tn(coef3[x], rows3[...])
        dist_ref[x] = new.reshape(NY, NZ, NV)
    for k in range(5):
        value = state[k * ROWS + NX : k * ROWS + 2 * NX, :]
        for y in range(NY):
            moved = value if y == 0 else pltpu.roll(value, CELLS - y * NZ, 1)
            macro_ref[k, :, y, :] = moved[:, 0:NZ]

    for it in range(ITERS):
        for copy in edge_copies(it):
            copy.wait_send()

        @pl.when(me < NCOMP)
        def _(it=it):
            for copy in near_copies(it):
                copy.wait_send()
            for step in range(1, n_vel):
                all_copy(it, step).wait_send()

        @pl.when(me == MASS)
        def _(it=it):
            for copy in tile_copies(it):
                copy.wait_send()
            for step in range(1, n_vel):
                mass_copy(it, step).wait_send()


def on_device(sizes, initial, velocity, weights, wall, wall_temp, mass_target):
    n_tx, n_ty, n_vel = sizes
    dma = pltpu.SemaphoreType.DMA
    vmem = pl.BlockSpec(memory_space=pltpu.VMEM)
    tiles = n_tx * n_ty - 1
    return pl.pallas_call(
        functools.partial(kernel, sizes),
        out_shape=(jax.ShapeDtypeStruct((NX, NY, NZ, NV), f32), jax.ShapeDtypeStruct((5, NX, NY, NZ), f32)),
        in_specs=[pl.BlockSpec(memory_space=pl.ANY), vmem, vmem, vmem, vmem, pl.BlockSpec(memory_space=pltpu.SMEM)],
        out_specs=(vmem, vmem),
        scratch_shapes=[
            pltpu.VMEM((ITERS, NX + 1, NY + 1, NZ, NV), f32),
            pltpu.VMEM((NX, NY, NZ, NV), f32),
            pltpu.VMEM((ITERS, NX, NZ, NV), f32),
            pltpu.VMEM((16 * NX, CELLS), f32),
            pltpu.VMEM((16 * NX, CELLS), f32),
            pltpu.VMEM((ITERS, n_vel - 1, NX, CELLS), f32),
            pltpu.VMEM((ITERS, 6, NX, CELLS), f32),
            pltpu.VMEM((ITERS, NCOMP, 6, NX, CELLS), f32),
            pltpu.VMEM((ITERS, tiles, NX, CELLS), f32),
            pltpu.VMEM((ITERS, NX, CELLS), f32),
            pltpu.VMEM((COEF * NX, CELLS), f32),
            pltpu.VMEM((NX, 128, CELLS), bf16),
            pltpu.VMEM((128, NV), f32),
            pltpu.VMEM((128, NV), bf16),
            pltpu.VMEM((16, NV), f32),
            pltpu.VMEM((32, NV), bf16),
            pltpu.VMEM((16, 128), bf16),
            pltpu.VMEM((8, NV), f32),
            pltpu.VMEM((NX, CELLS, 128), f32),
            pltpu.VMEM((1, NX, CELLS), f32),
            pltpu.VMEM((5 * ROWS, CELLS), f32),
            pltpu.VMEM((4 * ROWS, CELLS), f32),
            dma,
            dma((ITERS, n_vel - 1)), dma((ITERS, n_vel - 1)),
            dma((ITERS, 5)), dma((ITERS, 6)),
            dma((ITERS, n_vel - 1)), dma((ITERS, NCOMP)),
            dma((ITERS, tiles)), dma((ITERS, tiles)),
            dma((ITERS, n_vel - 1)), dma((ITERS,)),
            dma((ITERS, 3)), dma((ITERS, 3)),
        ],
        compiler_params=pltpu.CompilerParams(collective_id=0, has_side_effects=True, vmem_limit_bytes=48 * 1024 * 1024),
    )(initial, velocity, weights.reshape(1, -1), wall, wall_temp, mass_target.reshape(1, 1))


def solution(mesh):
    sizes = (mesh.shape["tx"], mesh.shape["ty"], mesh.shape["vel"])
    placed = (
        P("tx", "ty", None, "vel"),
        P(None, "vel"),
        P("vel"),
        P("tx", "ty", None),
        P("tx", "ty", None),
        P(),
    )
    return jax.shard_map(
        functools.partial(on_device, sizes),
        mesh=mesh,
        in_specs=placed,
        out_specs=(P("tx", "ty", None, "vel"), P(None, "tx", "ty", None)),
        check_vma=False,
    )
```

time: 445 us -> 83.9 us (0.19)
  the two profiles are of different devices: /device:TPU:8 before, /device:TPU:1 now
where the time goes in v1:
time: 83.9 us; the launch traced here: 83.5 us
  Pallas kernels  77 us (92%)
  local copies, waits for them, and re-layouts  5.24 us (6%)
  between operations  1.29 us (2%)
    pallas_call x1, Pallas kernels, on_device(): pl.pallas_call(functools.partial(kernel, sizes), out_shape=(jax.ShapeDtyp...  77 us
    unnamed x8, local copies, waits for them, and re-layouts  4.55 us

profile of v1, /device:TPU:1, one launch (start us, length us, event | category | flops | bytes accessed | tf_op | source)
XLA Modules:
  0.0 83.5 jit_solution(14813970455996920225)
XLA Ops:
  1.3 0.7 reshape.10.weight_ref
  2.0 0.0 copy-start
  2.0 0.8 copy-done
  2.7 0.0 copy-start.1
  2.7 0.8 copy-done.1
  3.5 0.0 copy-start.2
  3.5 0.7 copy-done.2
  4.2 77.0 %shard_map.77 = (f32[8,8,16,768]{3,2,1,0:T(8,128)S(1)}, f32[5,8,8,16]{3,2,1,0:T(8,128)S(1)}) custom-call(f32[8,8,16,768]{3,2,1,0:T(8,128)} %init_ref.1, f32[3,768]{1,0:T(4,128)S(1)} %copy-done.2, f32[1,768]{1,0:T(1,128)S(1)} %reshape.10.weight_ref, s32[8,8,16]{2,1,0:T(8,128)S(1)} %copy-done, f32[8,8,16]{2,1,0:T(8,128)S(1)} %copy-done.1, ...), custom_call_target="tpu_custom_call" | custom-call | tf_op jit(solution)/shard_map/pallas_call | solution.py:480
  81.2 1.7 %copy.11 = f32[8,8,16,768]{3,2,1,0:T(8,128)} copy(f32[8,8,16,768]{3,2,1,0:T(8,128)S(1)} %get-tuple-element.4) | data formatting | bytes 6291456
  82.9 0.7 copy.12
Async XLA Ops:
  2.0 0.8 copy-start
  2.7 0.8 copy-start.1
  3.5 0.7 copy-start.2

commit v2 on v1

v2 whole, which is shorter than its diff:
```python
import functools

import jax
import jax.numpy as jnp
from jax import lax
from jax.experimental import pallas as pl
from jax.experimental.pallas import tpu as pltpu
from jax.sharding import PartitionSpec as P

ITERS = 3
MACRO_STEPS = 4
SETS = 4
DEPTH = (4, 3, 3, 3)
SLOTS = {0: (0, 0), 1: (0, 1), 2: (0, 2), 3: (0, 3), 4: (1, 0), 5: (1, 1), 6: (1, 2),
         8: (2, 0), 9: (2, 1), 10: (2, 2), 11: (3, 0), 12: (3, 1), 13: (3, 2)}
MASS = 3
STEP = 0.1
f32 = jnp.float32
bf16 = jnp.bfloat16
MESH = pl.DeviceIdType.MESH
NX, NY, NZ, NV = 8, 8, 16, 768
CELLS = NY * NZ
ROWS = 48
PACE = (3, 6)
REACH = 5
COEF = 40
NEIGHBOURS = [(0, -1), (0, 1), (1, -1), (1, 0), (1, 1)]


def nt(a, b, precision=None):
    return lax.dot_general(a, b, (((1,), (1,)), ((), ())), precision=precision, preferred_element_type=f32)


def tn(a, b):
    return lax.dot_general(a, b, (((0,), (0,)), ((), ())), preferred_element_type=f32)


def rounded(value):
    return value.astype(bf16).astype(f32)


def lanes_of(value):
    return lax.broadcasted_iota(jnp.int32, value.shape, 1)


def other_half(value):
    parts = value.reshape(-1, 2, ROWS // 2, CELLS)
    return jnp.concatenate([parts[:, 1:2], parts[:, 0:1]], axis=1).reshape(value.shape)


def x_next(v):
    return pltpu.roll(v, v.shape[0] - 1, 0)


def x_last(v):
    return pltpu.roll(v, 1, 0)


def y_next(v):
    r = pltpu.roll(v, CELLS - NZ, 1)
    return jnp.where(lanes_of(v) < CELLS - NZ, r, other_half(r))


def y_last(v):
    r = pltpu.roll(v, NZ, 1)
    return jnp.where(lanes_of(v) >= NZ, r, other_half(r))


def z_next(v):
    z = lax.rem(lanes_of(v), NZ)
    return jnp.where(z == NZ - 1, pltpu.roll(v, NZ - 1, 1), pltpu.roll(v, CELLS - 1, 1))


def z_last(v):
    z = lax.rem(lanes_of(v), NZ)
    return jnp.where(z == 0, pltpu.roll(v, CELLS - NZ + 1, 1), pltpu.roll(v, 1, 1))


def field(v, k):
    return v[k * ROWS : (k + 1) * ROWS]


def kernel(
    sizes,
    init_ref, vel_in, weight_in, wall_in, wall_temp_in, target_ref,
    dist_ref, macro_ref,
    h, stream, edge_y, part, stream_part, rs, halves, gathered, tile_mass, mass,
    coef, coef3, rows_f, rows3, proj_f, proj2, mixed3, factors, open_cells, wall_rows, state, source,
    vel_ref, weight_ref, wall_ref, wall_temp_ref,
    load_sem, small_sem, rs_send, rs_recv, half_send, half_recv, all_send, all_recv,
    tile_send, tile_recv, mass_send, mass_recv, edge_send, edge_recv,
):
    n_tx, n_ty, n_vel = sizes
    tx, ty, me = lax.axis_index("tx"), lax.axis_index("ty"), lax.axis_index("vel")
    high_bit, low_bit = lax.rem(me // 4, 2), lax.rem(me, 2)
    my_set = high_bit * 2 + low_bit
    base = me - high_bit * 4 - low_bit

    def device(dx, dy, vel):
        return {"tx": lax.rem(tx + (dx + n_tx), n_tx), "ty": lax.rem(ty + dy, n_ty), "vel": vel}

    middle_bit = lax.rem(me // 2, 2)
    across = me + 2 - 4 * middle_bit
    ring = n_vel // 2
    my_place = me // 4 * 2 + low_bit

    def place_of(step):
        return lax.rem(my_place + step, ring)

    def group(step):
        at = place_of(step)
        return at // 2 * 4 + middle_bit * 2 + lax.rem(at, 2)

    def set_of(vel):
        return lax.rem(vel // 4, 2) * 2 + lax.rem(vel, 2)

    def mate(a, b):
        return base + lax.rem(high_bit + a, 2) * 4 + lax.rem(low_bit + b, 2)

    mates = [(0, 1), (1, 0), (1, 1)]
    far_tiles = [(a, b) for b in range(n_ty) for a in range(n_tx) if (a, b) != (0, 0)]
    near_tiles = [(dx % n_tx, dy) for dy, dx in NEIGHBOURS]
    only_far = [t for t in far_tiles if t not in near_tiles]

    loads = [pltpu.make_async_copy(init_ref.at[x], h.at[0, x, 0:NY], load_sem.at[x]) for x in range(NX)]
    smalls = [pltpu.make_async_copy(a, b, small_sem.at[at]) for at, (a, b) in enumerate(
        ((vel_in, vel_ref), (weight_in, weight_ref), (wall_in, wall_ref), (wall_temp_in, wall_temp_ref)))]
    for copy in smalls + loads:
        copy.start()

    barrier = pltpu.get_barrier_semaphore()
    for step in range(1, ring):
        pl.semaphore_signal(barrier, inc=1, device_id=device(0, 0, group(step)), device_id_type=MESH)
    pl.semaphore_signal(barrier, inc=1, device_id=device(0, 0, across), device_id_type=MESH)
    for a, b in [(0, 0)] + mates:
        for dx, dy in near_tiles:
            pl.semaphore_signal(barrier, inc=1, device_id=device(dx, dy, mate(a, b)), device_id_type=MESH)

    @pl.when(my_set == MASS)
    def _():
        for a, b in only_far:
            pl.semaphore_signal(barrier, inc=1, device_id=device(a, b, me), device_id_type=MESH)

    smalls[0].wait()
    smalls[1].wait()

    vx, vy, vz = vel_ref[0:1, :], vel_ref[1:2, :], vel_ref[2:3, :]
    speed_sq = vx * vx + vy * vy + vz * vz
    ones = jnp.ones_like(vx)
    basis = [ones, 2.0 * vx, 2.0 * vy, 2.0 * vz, speed_sq - 1.5]
    sides = []
    for v in (vx, vy, vz):
        sides += [STEP * jnp.maximum(v, 0.0), -STEP * jnp.minimum(v, 0.0)]
    scale = weight_ref[0:1, :] / float(NV * n_vel)
    none = jnp.zeros_like(vx)
    moments = [ones, vx, vy, vz,
               (2.0 / 3.0) * speed_sq - 1.0, 2.0 * (vx * vx - speed_sq / 3.0), 2.0 * (vy * vy - speed_sq / 3.0), none,
               2.0 * vx * vy, 2.0 * vx * vz, 2.0 * vy * vz, none,
               vx * (speed_sq - 2.5), vy * (speed_sq - 2.5), vz * (speed_sq - 2.5), ones]
    for at, row in enumerate(moments):
        proj_f[at : at + 1, :] = row * scale
    proj = proj_f[...]
    proj2[...] = jnp.concatenate([rounded(proj), proj - rounded(proj)], axis=0).astype(bf16)

    def prepare():
        rows = basis + [side * b for side in sides for b in basis] + [basis[4]]
        for copy in range(3):
            for at, row in enumerate(rows):
                rows_f[copy * COEF + at : copy * COEF + at + 1, :] = row
            rows_f[copy * COEF + len(rows) : (copy + 1) * COEF, :] = jnp.zeros((COEF - len(rows), NV), f32)
        rows_f[3 * COEF :, :] = jnp.zeros((128 - 3 * COEF, NV), f32)
        bx, by, bz = (STEP * jnp.abs(v) for v in (vx, vy, vz))
        for at, row in enumerate((0.9 - bx - by - bz, bx, by, bz, vz)):
            factors[at : at + 1, :] = row
        every = rows_f[...]
        high = rounded(every)
        rows3[...] = jnp.where(lax.broadcasted_iota(jnp.int32, every.shape, 0) < 2 * COEF, high, every - high).astype(bf16)
        mixed = nt(proj_f[...], every, lax.Precision.HIGHEST)
        mixed_high = rounded(mixed)
        mixed3[...] = jnp.where(lanes_of(mixed) < 2 * COEF, mixed_high, mixed - mixed_high).astype(bf16)

        smalls[2].wait()
        smalls[3].wait()
        solid = jnp.zeros((NX, CELLS), f32)
        heat = jnp.zeros((NX, CELLS), f32)
        for y in range(NY):
            spread = (lax.broadcasted_iota(jnp.int32, (NZ, CELLS), 1)
                      == lax.broadcasted_iota(jnp.int32, (NZ, CELLS), 0) + y * NZ).astype(f32)
            is_wall = (wall_ref[:, y, :] == 1).astype(f32)
            solid = solid + lax.dot_general(is_wall, spread, (((1,), (0,)), ((), ())), precision=lax.Precision.HIGHEST,
                                            preferred_element_type=f32)
            heat = heat + lax.dot_general(is_wall * wall_temp_ref[:, y, :], spread, (((1,), (0,)), ((), ())),
                                          precision=lax.Precision.HIGHEST, preferred_element_type=f32)
        fluid = 1.0 - solid
        wall_rows[0] = fluid
        for x in range(NX):
            open_cells[x] = jnp.broadcast_to(fluid[x : x + 1], (CELLS, CELLS)).T
        coef[35 * NX : 36 * NX, :] = heat
        coef[36 * NX :, :] = jnp.zeros((4 * NX, CELLS), f32)

    def projected(value):
        top = value.astype(bf16)
        low = (value - top.astype(f32)).astype(bf16)
        both = nt(proj2[...], top)
        return both[0:16] + both[16:32] + nt(proj2[0:16, :], low)

    def plane(it, x):
        return h[it, x, 0:NY].reshape(CELLS, NV)

    def pack_edge(it, x):
        top, bottom = h[it, x, NY - 1], h[it, x, 0]
        for t in range(6):
            cut = slice(t * 128, (t + 1) * 128)
            if t in (0, 3):
                piece = top[:, cut]
            elif t in (2, 5):
                piece = bottom[:, cut]
            else:
                piece = jnp.where(lanes_of(top[:, cut]) < 64, top[:, cut], bottom[:, cut])
            edge_y[it, x, :, cut] = piece

    def ordered(at):
        return lax.rem(at * (NX - 1), NX)

    def y_copy(it, x):
        return pltpu.make_async_remote_copy(
            src_ref=edge_y.at[it, x], dst_ref=h.at[it, x, NY],
            send_sem=edge_send.at[it, x], recv_sem=edge_recv.at[it, x],
            device_id=device(0, 1, me), device_id_type=MESH)

    def x_copies(it):
        half = NV // 2
        return [
            pltpu.make_async_remote_copy(
                src_ref=h.at[it, 0, 0:NY, :, half:NV], dst_ref=h.at[it, NX, 0:NY, :, half:NV],
                send_sem=edge_send.at[it, NX], recv_sem=edge_recv.at[it, NX],
                device_id=device(-1, 0, me), device_id_type=MESH),
            pltpu.make_async_remote_copy(
                src_ref=h.at[it, NX - 1, 0:NY, :, 0:half], dst_ref=h.at[it, NX, 0:NY, :, 0:half],
                send_sem=edge_send.at[it, NX + 1], recv_sem=edge_recv.at[it, NX + 1],
                device_id=device(1, 0, me), device_id_type=MESH),
        ]

    def send_edges(it, fill):
        def body(at, _):
            x = ordered(at)
            fill(x)
            pack_edge(it, x)
            pl.when(at < PACE[0])(y_copy(it, x).start)
            return 0

        lax.fori_loop(0, 2, body, 0)
        for copy in x_copies(it):
            copy.start()
        lax.fori_loop(2, NX, body, 0)

    def send_more(it, first, last):
        def body(at, _):
            y_copy(it, ordered(at)).start()
            return 0

        lax.fori_loop(first, last, body, 0)

    def stream_cell(it, x, y):
        half = NV // 2
        x_down, x_up = lax.rem(x + NX, NX + 1), x + 1
        y_down, y_up = (y + NY) % (NY + 1), y + 1
        for t in range(6):
            cut = slice(t * 128, (t + 1) * 128)
            own = h[it, x, y, :, cut]
            from_x = h[it, x_down if t < 3 else x_up, y, :, cut]
            if t in (0, 3):
                from_y = h[it, x, y_down, :, cut]
            elif t in (2, 5):
                from_y = h[it, x, y_up, :, cut]
            else:
                from_y = jnp.where(lanes_of(own) < 64, h[it, x, y_down, :, cut], h[it, x, y_up, :, cut])
            up = jnp.broadcast_to(factors[4:5, cut], own.shape) > 0.0
            from_z = jnp.where(up, pltpu.roll(own, 1, 0), pltpu.roll(own, NZ - 1, 0))
            value = (factors[0:1, cut] * own + factors[1:2, cut] * from_x
                     + factors[2:3, cut] * from_y + factors[3:4, cut] * from_z)
            stream[x, y, :, cut] = value * open_cells[x, y * NZ : (y + 1) * NZ, :]

    def stream_inside(it):
        def body(x, _):
            for y in range(1, NY - 1):
                stream_cell(it, x, y)
            return 0

        lax.fori_loop(1, NX - 1, body, 0)

    def stream_ends(it):
        for copy in x_copies(it):
            copy.wait_recv()

        def body(side, _):
            for y in range(1, NY - 1):
                stream_cell(it, side * (NX - 1), y)
            return 0

        lax.fori_loop(0, 2, body, 0)

    def stream_sides(it):
        def body(at, _):
            x = ordered(at)
            y_copy(it, x).wait_recv()
            stream_cell(it, x, 0)
            stream_cell(it, x, NY - 1)
            if it + 1 < ITERS:
                stream_part[pl.ds(x, 16, stride=NX), :] = projected(stream[x].reshape(CELLS, NV))
            return 0

        lax.fori_loop(0, NX, body, 0)

    def rs_copy(it, step):
        target = group(step)
        return pltpu.make_async_remote_copy(
            src_ref=part.at[pl.ds(pl.multiple_of(set_of(target) * 4 * NX, 4 * NX), 4 * NX)], dst_ref=rs.at[it, my_place],
            send_sem=rs_send.at[it, step - 1], recv_sem=rs_recv.at[it, my_place],
            device_id=device(0, 0, target), device_id_type=MESH)

    def rs_wait(it, step):
        at = place_of(step)
        pltpu.make_async_remote_copy(
            src_ref=part.at[0 : 4 * NX], dst_ref=rs.at[it, at],
            send_sem=rs_send.at[it, step - 1], recv_sem=rs_recv.at[it, at],
            device_id=device(0, 0, group(step)), device_id_type=MESH).wait_recv()

    def half_copy(it):
        return pltpu.make_async_remote_copy(
            src_ref=halves.at[it, 0], dst_ref=halves.at[it, 1],
            send_sem=half_send.at[it], recv_sem=half_recv.at[it],
            device_id=device(0, 0, across), device_id_type=MESH)

    def all_copies(it, depth):
        copies = []
        for a, b in [(0, 0)] + mates:
            for dy, dx in [(0, 0)] + NEIGHBOURS:
                if (a, b, dx, dy) == (0, 0, 0, 0):
                    continue
                slot = dy * 3 + 1 - dx
                cut = slice(0, 8) if dx == 0 else slice(8 - REACH, 8) if dx == 1 else slice(0, REACH)
                copies.append(pltpu.make_async_remote_copy(
                    src_ref=gathered.at[it, my_set, 1, 0:depth, cut], dst_ref=gathered.at[it, my_set, slot, 0:depth, cut],
                    send_sem=all_send.at[it, len(copies)], recv_sem=all_recv.at[it, my_set, slot],
                    device_id=device(dx, dy, mate(a, b)), device_id_type=MESH))
        return copies

    def for_depth(action):
        for depth in sorted(set(DEPTH)):
            wanted = [at for at in range(SETS) if DEPTH[at] == depth]
            match = my_set == wanted[0]
            for at in wanted[1:]:
                match = jnp.logical_or(match, my_set == at)

            @pl.when(match)
            def _(depth=depth):
                action(depth)

    def wait_all(it):
        for at in range(SETS):
            for slot in range(6):
                dx = 1 - slot % 3
                cut = slice(0, 8) if dx == 0 else slice(8 - REACH, 8) if dx == 1 else slice(0, REACH)

                def wait(at=at, slot=slot, cut=cut):
                    pltpu.make_async_remote_copy(
                        src_ref=gathered.at[it, at, 1, 0 : DEPTH[at], cut],
                        dst_ref=gathered.at[it, at, slot, 0 : DEPTH[at], cut],
                        send_sem=all_send.at[it, 0], recv_sem=all_recv.at[it, at, slot],
                        device_id=device(0, 0, group(1)), device_id_type=MESH).wait_recv()

                if slot == 1:
                    pl.when(my_set != at)(wait)
                else:
                    wait()

    def tile_copies(it):
        return [
            pltpu.make_async_remote_copy(
                src_ref=gathered.at[it, my_set, 1, 3], dst_ref=tile_mass.at[it, at],
                send_sem=tile_send.at[it, at], recv_sem=tile_recv.at[it, at],
                device_id=device(a, b, me), device_id_type=MESH)
            for at, (a, b) in enumerate(far_tiles)
        ]

    def mass_copies(it):
        return [
            pltpu.make_async_remote_copy(
                src_ref=mass.at[it], dst_ref=mass.at[it],
                send_sem=mass_send.at[it, at], recv_sem=mass_recv.at[it],
                device_id=device(0, 0, mate(a, b)), device_id_type=MESH)
            for at, (a, b) in enumerate(mates)
        ]

    def macro_solve(it):
        def g(c):
            if c == 7:
                return -(g(5) + g(6))
            at, k = SLOTS[c]
            return gathered[it, at, :, k].reshape(ROWS, CELLS)

        def many(*cs):
            return jnp.concatenate([g(c) for c in cs], axis=0)

        flow = many(1, 2, 3, 4)
        along = (many(5, 8, 9, 11), many(8, 6, 10, 12), many(9, 10, 7, 13))
        shifts = ((x_next, x_last), (y_next, y_last), (z_next, z_last))
        total = -6.0 * flow
        for (after, before), a in zip(shifts, along):
            total = total + (after(flow + 0.5 * a) + before(flow - 0.5 * a))
        source[0 : 3 * ROWS] = -0.5 * total[0 : 3 * ROWS]
        source[3 * ROWS :] = -(2.0 / 3.0) * total[3 * ROWS :]
        state[...] = many(0, 1, 2, 3, 4)

        def sweep(_, carry):
            rho, flow = state[0:ROWS], state[ROWS : 5 * ROWS]
            stack = jnp.concatenate([rho + field(flow, 3), flow], axis=0)
            laplace = -6.0 * flow
            grads, divergence = [], None
            for d, (after, before) in enumerate(shifts):
                up, down = after(stack), before(stack)
                laplace = laplace + (up[ROWS:] + down[ROWS:])
                grads.append(0.5 * (field(up, 0) - field(down, 0)))
                part_div = 0.5 * (field(up, 1 + d) - field(down, 1 + d))
                divergence = part_div if divergence is None else divergence + part_div
            state[0:ROWS] = rho - STEP * divergence
            for d in range(3):
                state[(1 + d) * ROWS : (2 + d) * ROWS] = field(flow, d) + STEP * (
                    -0.5 * grads[d] + 0.5 * field(laplace, d) + source[d * ROWS : (d + 1) * ROWS])
            state[4 * ROWS :] = field(flow, 3) + STEP * (
                -(2.0 / 3.0) * divergence + (2.0 / 3.0) * field(laplace, 3) + source[3 * ROWS :])
            return carry

        lax.fori_loop(0, MACRO_STEPS, sweep, 0)

    def coefficients(it):
        shift = target_ref[0, 0] - jnp.sum(mass[it]) / float(NX * NY * NZ * n_tx * n_ty)
        state[0:ROWS] = state[0:ROWS] + shift
        now = state[...]
        was = jnp.concatenate([gathered[it, SLOTS[c][0], :, SLOTS[c][1]].reshape(ROWS, CELLS) for c in range(5)], axis=0)
        change = now - was
        fluid = wall_rows[0]

        def own(value):
            return value.reshape(5, 2, ROWS // 2, CELLS)[:, 0, NX : 2 * NX]

        def put(at, value):
            coef[at * 5 * NX : (at + 1) * 5 * NX, :] = (value * fluid[None]).reshape(5 * NX, CELLS)

        here = own(change)
        put(0, 0.9 * here + STEP * own(now))
        for at, shift_of in enumerate((x_last, x_next, y_last, y_next, z_last, z_next)):
            put(1 + at, own(shift_of(change)) - here)
        for x in range(NX):
            c = coef[pl.ds(x, COEF, stride=NX), :]
            c_high = rounded(c)
            coef3[x] = jnp.concatenate([c_high, c - c_high, c_high, jnp.zeros((8, CELLS), f32)], axis=0).astype(bf16)

    def place(it, x, value):
        part[pl.ds(x, 16, stride=NX), :] = value

    for it in range(ITERS):
        if it == 0:
            for x in range(NX):
                loads[x].wait()
                place(0, x, projected(plane(0, x)))
            greeted = ring + 4 * len(near_tiles)

            @pl.when(my_set == MASS)
            def _():
                pl.semaphore_wait(barrier, greeted + len(only_far))

            @pl.when(my_set != MASS)
            def _():
                pl.semaphore_wait(barrier, greeted)

        for step in range(1, ring):
            rs_copy(it, step).start()

        def finalize(x, it=it):
            if it > 0:
                new = stream[x].reshape(CELLS, NV) + tn(coef3[x], rows3[...])
                h[it, x, 0:NY] = new.reshape(NY, NZ, NV)

        send_edges(it, finalize)
        if it == 0:
            prepare()

        rs[it, my_place] = part[pl.ds(pl.multiple_of(my_set * 4 * NX, 4 * NX), 4 * NX), :]
        for step in range(1, ring):
            rs_wait(it, step)
        total = rs[it, 0]
        for at in range(1, ring):
            total = total + rs[it, at]
        halves[it, 0] = total
        half_copy(it).start()
        send_more(it, PACE[0], PACE[1])
        stream_inside(it)
        half_copy(it).wait_recv()
        gathered[it, my_set, 1] = (total + halves[it, 1]).reshape(4, NX, CELLS)

        @pl.when(my_set == MASS)
        def _(it=it):
            for copy in tile_copies(it):
                copy.start()

        def send_all(depth, it=it):
            for copy in all_copies(it, depth):
                copy.start()

        for_depth(send_all)
        send_more(it, PACE[1], NX)

        @pl.when(my_set == MASS)
        def _(it=it):
            total = gathered[it, my_set, 1, 3]
            for at, copy in enumerate(tile_copies(it)):
                copy.wait_recv()
                total = total + tile_mass[it, at]
            mass[it] = total
            for copy in mass_copies(it):
                copy.start()

        stream_ends(it)
        stream_sides(it)
        wait_all(it)
        macro_solve(it)

        @pl.when(my_set != MASS)
        def _(it=it):
            mass_copies(it)[0].wait_recv()

        coefficients(it)

        for step in range(1, ring):
            rs_copy(it, step).wait_send()
        if it + 1 < ITERS:
            for x in range(NX):
                at = pl.ds(x, 16, stride=NX)
                part[at, :] = stream_part[at, :] + jnp.dot(mixed3[...], coef3[x], preferred_element_type=f32)

    for x in range(NX):
        new = stream[x].reshape(CELLS, NV) + tn(coef3[x], rows3[...])
        dist_ref[x] = new.reshape(NY, NZ, NV)
    for k in range(5):
        value = state[k * ROWS + NX : k * ROWS + 2 * NX, :]
        for y in range(NY):
            moved = value if y == 0 else pltpu.roll(value, CELLS - y * NZ, 1)
            macro_ref[k, :, y, :] = moved[:, 0:NZ]

    for it in range(ITERS):
        half_copy(it).wait_send()
        for copy in x_copies(it):
            copy.wait_send()

        def sent(x, _, it=it):
            y_copy(it, x).wait_send()
            return 0

        lax.fori_loop(0, NX, sent, 0)

        def sent_all(depth, it=it):
            for copy in all_copies(it, depth):
                copy.wait_send()

        for_depth(sent_all)

        @pl.when(my_set == MASS)
        def _(it=it):
            for copy in tile_copies(it):
                copy.wait_send()
            for copy in mass_copies(it):
                copy.wait_send()


def on_device(sizes, initial, velocity, weights, wall, wall_temp, mass_target):
    n_tx, n_ty, n_vel = sizes
    dma = pltpu.SemaphoreType.DMA
    vmem = pl.BlockSpec(memory_space=pltpu.VMEM)
    tiles = n_tx * n_ty - 1
    return pl.pallas_call(
        functools.partial(kernel, sizes),
        out_shape=(jax.ShapeDtypeStruct((NX, NY, NZ, NV), f32), jax.ShapeDtypeStruct((5, NX, NY, NZ), f32)),
        in_specs=[pl.BlockSpec(memory_space=pltpu.HBM)] * 5 + [pl.BlockSpec(memory_space=pltpu.SMEM)],
        out_specs=(vmem, vmem),
        scratch_shapes=[
            pltpu.VMEM((ITERS, NX + 1, NY + 1, NZ, NV), f32),
            pltpu.VMEM((NX, NY, NZ, NV), f32),
            pltpu.VMEM((ITERS, NX, NZ, NV), f32),
            pltpu.VMEM((16 * NX, CELLS), f32),
            pltpu.VMEM((16 * NX, CELLS), f32),
            pltpu.VMEM((ITERS, n_vel // 2, 4 * NX, CELLS), f32),
            pltpu.VMEM((ITERS, 2, 4 * NX, CELLS), f32),
            pltpu.VMEM((ITERS, SETS, 6, 4, NX, CELLS), f32),
            pltpu.VMEM((ITERS, tiles, NX, CELLS), f32),
            pltpu.VMEM((ITERS, NX, CELLS), f32),
            pltpu.VMEM((COEF * NX, CELLS), f32),
            pltpu.VMEM((NX, 128, CELLS), bf16),
            pltpu.VMEM((128, NV), f32),
            pltpu.VMEM((128, NV), bf16),
            pltpu.VMEM((16, NV), f32),
            pltpu.VMEM((32, NV), bf16),
            pltpu.VMEM((16, 128), bf16),
            pltpu.VMEM((8, NV), f32),
            pltpu.VMEM((NX, CELLS, 128), f32),
            pltpu.VMEM((1, NX, CELLS), f32),
            pltpu.VMEM((5 * ROWS, CELLS), f32),
            pltpu.VMEM((4 * ROWS, CELLS), f32),
            pltpu.VMEM((3, NV), f32), pltpu.VMEM((1, NV), f32),
            pltpu.VMEM((NX, NY, NZ), jnp.int32), pltpu.VMEM((NX, NY, NZ), f32),
            dma((NX,)), dma((4,)),
            dma((ITERS, n_vel // 2 - 1)), dma((ITERS, n_vel // 2)),
            dma((ITERS,)), dma((ITERS,)),
            dma((ITERS, 23)), dma((ITERS, SETS, 6)),
            dma((ITERS, tiles)), dma((ITERS, tiles)),
            dma((ITERS, 3)), dma((ITERS,)),
            dma((ITERS, NX + 2)), dma((ITERS, NX + 2)),
        ],
        compiler_params=pltpu.CompilerParams(collective_id=0, has_side_effects=True, vmem_limit_bytes=48 * 1024 * 1024),
    )(initial, velocity, weights.reshape(1, -1), wall, wall_temp, mass_target.reshape(1, 1))


def solution(mesh):
    sizes = (mesh.shape["tx"], mesh.shape["ty"], mesh.shape["vel"])
    placed = (
        P("tx", "ty", None, "vel"),
        P(None, "vel"),
        P("vel"),
        P("tx", "ty", None),
        P("tx", "ty", None),
        P(),
    )
    return jax.shard_map(
        functools.partial(on_device, sizes),
        mesh=mesh,
        in_specs=placed,
        out_specs=(P("tx", "ty", None, "vel"), P(None, "tx", "ty", None)),
        check_vma=False,
    )
```

time: 83.9 us -> 69.2 us (0.82)
  Pallas kernels: 77 us -> 62.4 us
    pallas_call x1, Pallas kernels: 77 us -> 62.4 us  [on_device(): pl.pallas_call(functools.partial(kernel, sizes), out_shape=(jax.ShapeDtyp...]
where the time goes in v2:
time: 69.2 us; the launch traced here: 68.9 us
  Pallas kernels  62.4 us (90%)
  local copies, waits for them, and re-layouts  5.24 us (8%)
  between operations  1.29 us (2%)
    pallas_call x1, Pallas kernels, on_device(): pl.pallas_call(functools.partial(kernel, sizes), out_shape=(jax.ShapeDtyp...  62.4 us
    unnamed x8, local copies, waits for them, and re-layouts  4.55 us

profile of v2, /device:TPU:1, one launch (start us, length us, event | category | flops | bytes accessed | tf_op | source)
XLA Modules:
  0.0 68.9 jit_solution(10180843250837894641)
XLA Ops:
  1.3 0.7 %reshape.10.weight_in = f32[1,768]{1,0:T(1,128)S(1)} reshape(f32[768]{0:T(1024)} %param.8) | data formatting | bytes 6144 | tf_op jit(solution)/shard_map/reshape | solution.py:621
  2.0 0.0 copy-start
  2.0 0.8 %copy-done = s32[8,8,16]{2,1,0:T(8,128)S(1)} copy-done((s32[8,8,16]{2,1,0:T(8,128)S(1)}, s32[8,8,16]{2,1,0:T(8,128)}, u32[]{:S(2)}) %copy-start) | copy-done | bytes 4120
  2.7 0.0 copy-start.1
  2.7 0.8 %copy-done.1 = f32[8,8,16]{2,1,0:T(8,128)S(1)} copy-done((f32[8,8,16]{2,1,0:T(8,128)S(1)}, f32[8,8,16]{2,1,0:T(8,128)}, u32[]{:S(2)}) %copy-start.1) | copy-done | bytes 4120
  3.5 0.0 copy-start.2
  3.5 0.7 %copy-done.2 = f32[3,768]{1,0:T(4,128)S(1)} copy-done((f32[3,768]{1,0:T(4,128)S(1)}, f32[3,768]{1,0:T(4,128)}, u32[]{:S(2)}) %copy-start.2) | copy-done | bytes 9240
  4.2 62.4 %shard_map.77 = (f32[8,8,16,768]{3,2,1,0:T(8,128)S(1)}, f32[5,8,8,16]{3,2,1,0:T(8,128)S(1)}) custom-call(f32[8,8,16,768]{3,2,1,0:T(8,128)} %init_ref.1, f32[3,768]{1,0:T(4,128)S(1)} %copy-done.2, f32[1,768]{1,0:T(1,128)S(1)} %reshape.10.weight_in, s32[8,8,16]{2,1,0:T(8,128)S(1)} %copy-done, f32[8,8,16]{2,1,0:T(8,128)S(1)} %copy-done.1, f32[1,1]{1,0:T(1,128)} %bitcast.1.target_ref), custom_call_target="tpu_custom_call" | custom-call | tf_op jit(solution)/shard_map/pallas_call | solution.py:582
  66.5 1.7 %copy.11 = f32[8,8,16,768]{3,2,1,0:T(8,128)} copy(f32[8,8,16,768]{3,2,1,0:T(8,128)S(1)} %get-tuple-element.4) | data formatting | bytes 6291456
  68.2 0.7 copy.12
Async XLA Ops:
  2.0 0.8 %copy-start = (s32[8,8,16]{2,1,0:T(8,128)S(1)}, s32[8,8,16]{2,1,0:T(8,128)}, u32[]{:S(2)}) copy-start(s32[8,8,16]{2,1,0:T(8,128)} %wall_in.1) | copy-start | bytes 12292
  2.7 0.8 %copy-start.1 = (f32[8,8,16]{2,1,0:T(8,128)S(1)}, f32[8,8,16]{2,1,0:T(8,128)}, u32[]{:S(2)}) copy-start(f32[8,8,16]{2,1,0:T(8,128)} %wall_temp_in.1) | copy-start | bytes 12292
  3.5 0.7 %copy-start.2 = (f32[3,768]{1,0:T(4,128)S(1)}, f32[3,768]{1,0:T(4,128)}, u32[]{:S(2)}) copy-start(f32[3,768]{1,0:T(4,128)} %vel_in.1) | copy-start | bytes 27652

commit v3 on v2

--- a/solution.py
+++ b/solution.py
@@ -21,9 +21,11 @@
 NX, NY, NZ, NV = 8, 8, 16, 768
 CELLS = NY * NZ
 ROWS = 48
-PACE = (3, 6)
+PACE = (4, 7)
+EARLY = 6
 REACH = 5
 COEF = 40
+FAR_FIRST = [(1, -1), (1, 1), (0, -1), (0, 1), (1, 0), (0, 0)]
 NEIGHBOURS = [(0, -1), (0, 1), (1, -1), (1, 0), (1, 1)]
 
 
@@ -86,7 +88,7 @@
     dist_ref, macro_ref,
     h, stream, edge_y, part, stream_part, rs, halves, gathered, tile_mass, mass,
     coef, coef3, rows_f, rows3, proj_f, proj2, mixed3, factors, open_cells, wall_rows, state, source,
-    vel_ref, weight_ref, wall_ref, wall_temp_ref,
+    velocity_ref, weight_ref, wall_ref, wall_temp_ref,
     load_sem, small_sem, rs_send, rs_recv, half_send, half_recv, all_send, all_recv,
     tile_send, tile_recv, mass_send, mass_recv, edge_send, edge_recv,
 ):
@@ -124,7 +126,7 @@
 
     loads = [pltpu.make_async_copy(init_ref.at[x], h.at[0, x, 0:NY], load_sem.at[x]) for x in range(NX)]
     smalls = [pltpu.make_async_copy(a, b, small_sem.at[at]) for at, (a, b) in enumerate(
-        ((vel_in, vel_ref), (weight_in, weight_ref), (wall_in, wall_ref), (wall_temp_in, wall_temp_ref)))]
+        ((vel_in, velocity_ref), (weight_in, weight_ref), (wall_in, wall_ref), (wall_temp_in, wall_temp_ref)))]
     for copy in smalls + loads:
         copy.start()
 
@@ -143,15 +145,14 @@
 
     smalls[0].wait()
     smalls[1].wait()
-
-    vx, vy, vz = vel_ref[0:1, :], vel_ref[1:2, :], vel_ref[2:3, :]
+    vx, vy, vz = velocity_ref[0:1, :], velocity_ref[1:2, :], velocity_ref[2:3, :]
     speed_sq = vx * vx + vy * vy + vz * vz
     ones = jnp.ones_like(vx)
     basis = [ones, 2.0 * vx, 2.0 * vy, 2.0 * vz, speed_sq - 1.5]
     sides = []
     for v in (vx, vy, vz):
         sides += [STEP * jnp.maximum(v, 0.0), -STEP * jnp.minimum(v, 0.0)]
-    scale = weight_ref[0:1, :] / float(NV * n_vel)
+    scale = weight_ref[...].reshape(1, NV) / float(NV * n_vel)
     none = jnp.zeros_like(vx)
     moments = [ones, vx, vy, vz,
                (2.0 / 3.0) * speed_sq - 1.0, 2.0 * (vx * vx - speed_sq / 3.0), 2.0 * (vy * vy - speed_sq / 3.0), none,
@@ -163,22 +164,9 @@
     proj2[...] = jnp.concatenate([rounded(proj), proj - rounded(proj)], axis=0).astype(bf16)
 
     def prepare():
-        rows = basis + [side * b for side in sides for b in basis] + [basis[4]]
-        for copy in range(3):
-            for at, row in enumerate(rows):
-                rows_f[copy * COEF + at : copy * COEF + at + 1, :] = row
-            rows_f[copy * COEF + len(rows) : (copy + 1) * COEF, :] = jnp.zeros((COEF - len(rows), NV), f32)
-        rows_f[3 * COEF :, :] = jnp.zeros((128 - 3 * COEF, NV), f32)
         bx, by, bz = (STEP * jnp.abs(v) for v in (vx, vy, vz))
         for at, row in enumerate((0.9 - bx - by - bz, bx, by, bz, vz)):
             factors[at : at + 1, :] = row
-        every = rows_f[...]
-        high = rounded(every)
-        rows3[...] = jnp.where(lax.broadcasted_iota(jnp.int32, every.shape, 0) < 2 * COEF, high, every - high).astype(bf16)
-        mixed = nt(proj_f[...], every, lax.Precision.HIGHEST)
-        mixed_high = rounded(mixed)
-        mixed3[...] = jnp.where(lanes_of(mixed) < 2 * COEF, mixed_high, mixed - mixed_high).astype(bf16)
-
         smalls[2].wait()
         smalls[3].wait()
         solid = jnp.zeros((NX, CELLS), f32)
@@ -187,16 +175,31 @@
             spread = (lax.broadcasted_iota(jnp.int32, (NZ, CELLS), 1)
                       == lax.broadcasted_iota(jnp.int32, (NZ, CELLS), 0) + y * NZ).astype(f32)
             is_wall = (wall_ref[:, y, :] == 1).astype(f32)
-            solid = solid + lax.dot_general(is_wall, spread, (((1,), (0,)), ((), ())), precision=lax.Precision.HIGHEST,
-                                            preferred_element_type=f32)
-            heat = heat + lax.dot_general(is_wall * wall_temp_ref[:, y, :], spread, (((1,), (0,)), ((), ())),
-                                          precision=lax.Precision.HIGHEST, preferred_element_type=f32)
+            both = jnp.concatenate([is_wall, is_wall * wall_temp_ref[:, y, :]], axis=0)
+            moved = lax.dot_general(both, spread, (((1,), (0,)), ((), ())), precision=lax.Precision.HIGHEST,
+                                    preferred_element_type=f32)
+            solid = solid + moved[0:NX]
+            heat = heat + moved[NX:]
         fluid = 1.0 - solid
         wall_rows[0] = fluid
         for x in range(NX):
             open_cells[x] = jnp.broadcast_to(fluid[x : x + 1], (CELLS, CELLS)).T
         coef[35 * NX : 36 * NX, :] = heat
         coef[36 * NX :, :] = jnp.zeros((4 * NX, CELLS), f32)
+
+    def prepare_rows():
+        rows = basis + [side * b for side in sides for b in basis] + [basis[4]]
+        for copy in range(3):
+            for at, row in enumerate(rows):
+                rows_f[copy * COEF + at : copy * COEF + at + 1, :] = row
+            rows_f[copy * COEF + len(rows) : (copy + 1) * COEF, :] = jnp.zeros((COEF - len(rows), NV), f32)
+        rows_f[3 * COEF :, :] = jnp.zeros((128 - 3 * COEF, NV), f32)
+        every = rows_f[...]
+        high = rounded(every)
+        rows3[...] = jnp.where(lax.broadcasted_iota(jnp.int32, every.shape, 0) < 2 * COEF, high, every - high).astype(bf16)
+        mixed = nt(proj_f[...], every, lax.Precision.HIGHEST)
+        mixed_high = rounded(mixed)
+        mixed3[...] = jnp.where(lanes_of(mixed) < 2 * COEF, mixed_high, mixed - mixed_high).astype(bf16)
 
     def projected(value):
         top = value.astype(bf16)
@@ -300,7 +303,7 @@
 
         lax.fori_loop(0, 2, body, 0)
 
-    def stream_sides(it):
+    def stream_sides(it, first, last):
         def body(at, _):
             x = ordered(at)
             y_copy(it, x).wait_recv()
@@ -310,7 +313,7 @@
                 stream_part[pl.ds(x, 16, stride=NX), :] = projected(stream[x].reshape(CELLS, NV))
             return 0
 
-        lax.fori_loop(0, NX, body, 0)
+        lax.fori_loop(first, last, body, 0)
 
     def rs_copy(it, step):
         target = group(step)
@@ -334,8 +337,8 @@
 
     def all_copies(it, depth):
         copies = []
-        for a, b in [(0, 0)] + mates:
-            for dy, dx in [(0, 0)] + NEIGHBOURS:
+        for dy, dx in FAR_FIRST:
+            for a, b in mates[::-1] + [(0, 0)]:
                 if (a, b, dx, dy) == (0, 0, 0, 0):
                     continue
                 slot = dy * 3 + 1 - dx
@@ -512,6 +515,11 @@
         for_depth(send_all)
         send_more(it, PACE[1], NX)
 
+        if it == 0:
+            prepare_rows()
+        stream_ends(it)
+        stream_sides(it, 0, EARLY)
+
         @pl.when(my_set == MASS)
         def _(it=it):
             total = gathered[it, my_set, 1, 3]
@@ -522,10 +530,9 @@
             for copy in mass_copies(it):
                 copy.start()
 
-        stream_ends(it)
-        stream_sides(it)
         wait_all(it)
         macro_solve(it)
+        stream_sides(it, EARLY, NX)
 
         @pl.when(my_set != MASS)
         def _(it=it):
@@ -607,7 +614,7 @@
             pltpu.VMEM((1, NX, CELLS), f32),
             pltpu.VMEM((5 * ROWS, CELLS), f32),
             pltpu.VMEM((4 * ROWS, CELLS), f32),
-            pltpu.VMEM((3, NV), f32), pltpu.VMEM((1, NV), f32),
+            pltpu.VMEM((3, NV), f32), pltpu.VMEM((NV,), f32),
             pltpu.VMEM((NX, NY, NZ), jnp.int32), pltpu.VMEM((NX, NY, NZ), f32),
             dma((NX,)), dma((4,)),
             dma((ITERS, n_vel // 2 - 1)), dma((ITERS, n_vel // 2)),
@@ -618,7 +625,11 @@
             dma((ITERS, NX + 2)), dma((ITERS, NX + 2)),
         ],
         compiler_params=pltpu.CompilerParams(collective_id=0, has_side_effects=True, vmem_limit_bytes=48 * 1024 * 1024),
-    )(initial, velocity, weights.reshape(1, -1), wall, wall_temp, mass_target.reshape(1, 1))
+    )(
+        initial,
+        *(pltpu.with_memory_space_constraint(a, pltpu.HBM) for a in (velocity, weights, wall, wall_temp)),
+        mass_target.reshape(1, 1),
+    )
 
 
 def solution(mesh):

time: 69.2 us -> 63.5 us (0.918)
  local copies, waits for them, and re-layouts: 5.24 us -> 2.33 us
  Pallas kernels: 62.4 us -> 59.8 us
    pallas_call x1, Pallas kernels: 62.4 us -> 59.8 us  [on_device(): pl.pallas_call(functools.partial(kernel, sizes), out_shape=(jax.ShapeDtyp...]
    unnamed x8 -> x2, local copies, waits for them, and re-layouts: 4.55 us -> 2.33 us
where the time goes in v3:
time: 63.5 us; the launch traced here: 63.4 us
  Pallas kernels  59.8 us (94%)
  local copies, waits for them, and re-layouts  2.33 us (4%)
  between operations  1.29 us (2%)
    pallas_call x1, Pallas kernels, on_device(): pl.pallas_call(functools.partial(kernel, sizes), out_shape=(jax.ShapeDtyp...  59.8 us
    unnamed x2, local copies, waits for them, and re-layouts  2.33 us

profile of v3, /device:TPU:1, one launch (start us, length us, event | category | flops | bytes accessed | tf_op | source)
XLA Modules:
  0.0 63.4 jit_solution(4625081572036964438)
XLA Ops:
  1.3 59.8 %shard_map.77 = (f32[8,8,16,768]{3,2,1,0:T(8,128)S(1)}, f32[5,8,8,16]{3,2,1,0:T(8,128)S(1)}) custom-call(f32[8,8,16,768]{3,2,1,0:T(8,128)} %init_ref.1, f32[3,768]{1,0:T(4,128)} %vel_in.1, f32[768]{0:T(1024)} %weight_in.1, s32[8,8,16]{2,1,0:T(8,128)} %wall_in.1, f32[8,8,16]{2,1,0:T(8,128)} %wall_temp_in.1, f32[1,1]{1,0:T(1,128)} %bitcast.1.target_ref), custom_call_target="tpu_custom_call" | custom-call | tf_op jit(solution)/shard_map/pallas_call | solution.py:589
  61.0 1.7 %copy.11 = f32[8,8,16,768]{3,2,1,0:T(8,128)} copy(f32[8,8,16,768]{3,2,1,0:T(8,128)S(1)} %get-tuple-element.4) | data formatting | bytes 6291456
  62.7 0.7 %copy.12 = f32[5,8,8,16]{3,2,1,0:T(8,128)} copy(f32[5,8,8,16]{3,2,1,0:T(8,128)S(1)} %get-tuple-element.5) | data formatting | bytes 40960

commit v4 on v3

--- a/solution.py
+++ b/solution.py
@@ -29,6 +29,13 @@
 NEIGHBOURS = [(0, -1), (0, 1), (1, -1), (1, 0), (1, 1)]
 
 
+def rows_read(dx, dy):
+    if dx == 0:
+        return slice(0, NX)
+    reach = REACH - dy
+    return slice(NX - reach, NX) if dx == 1 else slice(0, reach)
+
+
 def nt(a, b, precision=None):
     return lax.dot_general(a, b, (((1,), (1,)), ((), ())), precision=precision, preferred_element_type=f32)
 
@@ -69,13 +76,11 @@
 
 
 def z_next(v):
-    z = lax.rem(lanes_of(v), NZ)
-    return jnp.where(z == NZ - 1, pltpu.roll(v, NZ - 1, 1), pltpu.roll(v, CELLS - 1, 1))
+    return jnp.where((lanes_of(v) & (NZ - 1)) == NZ - 1, pltpu.roll(v, NZ - 1, 1), pltpu.roll(v, CELLS - 1, 1))
 
 
 def z_last(v):
-    z = lax.rem(lanes_of(v), NZ)
-    return jnp.where(z == 0, pltpu.roll(v, CELLS - NZ + 1, 1), pltpu.roll(v, 1, 1))
+    return jnp.where((lanes_of(v) & (NZ - 1)) == 0, pltpu.roll(v, CELLS - NZ + 1, 1), pltpu.roll(v, 1, 1))
 
 
 def field(v, k):
@@ -86,7 +91,7 @@
     sizes,
     init_ref, vel_in, weight_in, wall_in, wall_temp_in, target_ref,
     dist_ref, macro_ref,
-    h, stream, edge_y, part, stream_part, rs, halves, gathered, tile_mass, mass,
+    h, stream, edge_y, part, stream_part, rs, halves, gathered, tile_row, tile_mass, mass,
     coef, coef3, rows_f, rows3, proj_f, proj2, mixed3, factors, open_cells, wall_rows, state, source,
     velocity_ref, weight_ref, wall_ref, wall_temp_ref,
     load_sem, small_sem, rs_send, rs_recv, half_send, half_recv, all_send, all_recv,
@@ -342,7 +347,7 @@
                 if (a, b, dx, dy) == (0, 0, 0, 0):
                     continue
                 slot = dy * 3 + 1 - dx
-                cut = slice(0, 8) if dx == 0 else slice(8 - REACH, 8) if dx == 1 else slice(0, REACH)
+                cut = rows_read(dx, dy)
                 copies.append(pltpu.make_async_remote_copy(
                     src_ref=gathered.at[it, my_set, 1, 0:depth, cut], dst_ref=gathered.at[it, my_set, slot, 0:depth, cut],
                     send_sem=all_send.at[it, len(copies)], recv_sem=all_recv.at[it, my_set, slot],
@@ -364,7 +369,7 @@
         for at in range(SETS):
             for slot in range(6):
                 dx = 1 - slot % 3
-                cut = slice(0, 8) if dx == 0 else slice(8 - REACH, 8) if dx == 1 else slice(0, REACH)
+                cut = rows_read(dx, slot // 3)
 
                 def wait(at=at, slot=slot, cut=cut):
                     pltpu.make_async_remote_copy(
@@ -381,7 +386,7 @@
     def tile_copies(it):
         return [
             pltpu.make_async_remote_copy(
-                src_ref=gathered.at[it, my_set, 1, 3], dst_ref=tile_mass.at[it, at],
+                src_ref=tile_row.at[it], dst_ref=tile_mass.at[it, at],
                 send_sem=tile_send.at[it, at], recv_sem=tile_recv.at[it, at],
                 device_id=device(a, b, me), device_id_type=MESH)
             for at, (a, b) in enumerate(far_tiles)
@@ -445,16 +450,25 @@
         change = now - was
         fluid = wall_rows[0]
 
-        def own(value):
-            return value.reshape(5, 2, ROWS // 2, CELLS)[:, 0, NX : 2 * NX]
+        def tile(value, half):
+            return value.reshape(5, 2, ROWS // 2, CELLS)[:, half, NX : 2 * NX].reshape(5 * NX, CELLS)
+
+        def along_x(value):
+            return value.reshape(5, ROWS // 2, CELLS)[:, NX : 2 * NX].reshape(5 * NX, CELLS)
 
         def put(at, value):
-            coef[at * 5 * NX : (at + 1) * 5 * NX, :] = (value * fluid[None]).reshape(5 * NX, CELLS)
-
-        here = own(change)
-        put(0, 0.9 * here + STEP * own(now))
-        for at, shift_of in enumerate((x_last, x_next, y_last, y_next, z_last, z_next)):
-            put(1 + at, own(shift_of(change)) - here)
+            coef[at * 5 * NX : (at + 1) * 5 * NX, :] = (value.reshape(5, NX, CELLS) * fluid[None]).reshape(5 * NX, CELLS)
+
+        here, other = tile(change, 0), tile(change, 1)
+        strip = change.reshape(5, 2, ROWS // 2, CELLS)[:, 0].reshape(5 * ROWS // 2, CELLS)
+        lane = lanes_of(here)
+        put(0, 0.9 * here + STEP * tile(now, 0))
+        put(1, along_x(x_last(strip)) - here)
+        put(2, along_x(x_next(strip)) - here)
+        put(3, jnp.where(lane >= NZ, pltpu.roll(here, NZ, 1), pltpu.roll(other, NZ, 1)) - here)
+        put(4, jnp.where(lane < CELLS - NZ, pltpu.roll(here, CELLS - NZ, 1), pltpu.roll(other, CELLS - NZ, 1)) - here)
+        put(5, z_last(here) - here)
+        put(6, z_next(here) - here)
         for x in range(NX):
             c = coef[pl.ds(x, COEF, stride=NX), :]
             c_high = rounded(c)
@@ -503,16 +517,18 @@
         half_copy(it).wait_recv()
         gathered[it, my_set, 1] = (total + halves[it, 1]).reshape(4, NX, CELLS)
 
-        @pl.when(my_set == MASS)
-        def _(it=it):
-            for copy in tile_copies(it):
-                copy.start()
-
         def send_all(depth, it=it):
             for copy in all_copies(it, depth):
                 copy.start()
 
         for_depth(send_all)
+
+        @pl.when(my_set == MASS)
+        def _(it=it):
+            tile_row[it] = jnp.sum(gathered[it, my_set, 1, 3], axis=0, keepdims=True)
+            for copy in tile_copies(it):
+                copy.start()
+
         send_more(it, PACE[1], NX)
 
         if it == 0:
@@ -522,7 +538,7 @@
 
         @pl.when(my_set == MASS)
         def _(it=it):
-            total = gathered[it, my_set, 1, 3]
+            total = tile_row[it]
             for at, copy in enumerate(tile_copies(it)):
                 copy.wait_recv()
                 total = total + tile_mass[it, at]
@@ -600,8 +616,9 @@
             pltpu.VMEM((ITERS, n_vel // 2, 4 * NX, CELLS), f32),
             pltpu.VMEM((ITERS, 2, 4 * NX, CELLS), f32),
             pltpu.VMEM((ITERS, SETS, 6, 4, NX, CELLS), f32),
-            pltpu.VMEM((ITERS, tiles, NX, CELLS), f32),
-            pltpu.VMEM((ITERS, NX, CELLS), f32),
+            pltpu.VMEM((ITERS, 1, CELLS), f32),
+            pltpu.VMEM((ITERS, tiles, 1, CELLS), f32),
+            pltpu.VMEM((ITERS, 1, CELLS), f32),
             pltpu.VMEM((COEF * NX, CELLS), f32),
             pltpu.VMEM((NX, 128, CELLS), bf16),
             pltpu.VMEM((128, NV), f32),

time: 63.5 us -> 62.7 us (0.987)
  Pallas kernels: 59.8 us -> 59 us
    pallas_call x1, Pallas kernels: 59.8 us -> 59 us  [on_device(): pl.pallas_call(functools.partial(kernel, sizes), out_shape=(jax.ShapeDtyp...]
where the time goes in v4:
time: 62.7 us; the launch traced here: 62.6 us
  Pallas kernels  59 us (94%)
  local copies, waits for them, and re-layouts  2.33 us (4%)
  between operations  1.29 us (2%)
    pallas_call x1, Pallas kernels, on_device(): pl.pallas_call(functools.partial(kernel, sizes), out_shape=(jax.ShapeDtyp...  59 us
    unnamed x2, local copies, waits for them, and re-layouts  2.33 us

profile of v4, /device:TPU:1, one launch (start us, length us, event | category | flops | bytes accessed | tf_op | source)
XLA Modules:
  0.0 62.6 jit_solution(3614076827494811002)
XLA Ops:
  1.3 59.0 %shard_map.77 = (f32[8,8,16,768]{3,2,1,0:T(8,128)S(1)}, f32[5,8,8,16]{3,2,1,0:T(8,128)S(1)}) custom-call(f32[8,8,16,768]{3,2,1,0:T(8,128)} %init_ref.1, f32[3,768]{1,0:T(4,128)} %vel_in.1, f32[768]{0:T(1024)} %weight_in.1, s32[8,8,16]{2,1,0:T(8,128)} %wall_in.1, f32[8,8,16]{2,1,0:T(8,128)} %wall_temp_in.1, f32[1,1]{1,0:T(1,128)} %bitcast.1.target_ref), custom_call_target="tpu_custom_call" | custom-call | tf_op jit(solution)/shard_map/pallas_call | solution.py:605
  60.3 1.7 %copy.11 = f32[8,8,16,768]{3,2,1,0:T(8,128)} copy(f32[8,8,16,768]{3,2,1,0:T(8,128)S(1)} %get-tuple-element.4) | data formatting | bytes 6291456
  61.9 0.7 %copy.12 = f32[5,8,8,16]{3,2,1,0:T(8,128)} copy(f32[5,8,8,16]{3,2,1,0:T(8,128)S(1)} %get-tuple-element.5) | data formatting | bytes 40960

commit v5 on v4

--- a/solution.py
+++ b/solution.py
@@ -492,7 +492,7 @@
             def _():
                 pl.semaphore_wait(barrier, greeted)
 
-        for step in range(1, ring):
+        for step in sorted(range(1, ring), key=lambda at: abs(at - ring // 2)):
             rs_copy(it, step).start()
 
         def finalize(x, it=it):

time: 62.7 us -> 62.5 us (level)
  no operation moved by 1% of the time
where the time goes in v5:
time: 62.5 us; the launch traced here: 62.4 us
  Pallas kernels  58.8 us (94%)
  local copies, waits for them, and re-layouts  2.33 us (4%)
  between operations  1.29 us (2%)
    pallas_call x1, Pallas kernels, on_device(): pl.pallas_call(functools.partial(kernel, sizes), out_shape=(jax.ShapeDtyp...  58.8 us
    unnamed x2, local copies, waits for them, and re-layouts  2.33 us

profile of v5, /device:TPU:1, one launch (start us, length us, event | category | flops | bytes accessed | tf_op | source)
XLA Modules:
  0.0 62.4 jit_solution(18120581887988646980)
XLA Ops:
  1.3 58.8 %shard_map.77 = (f32[8,8,16,768]{3,2,1,0:T(8,128)S(1)}, f32[5,8,8,16]{3,2,1,0:T(8,128)S(1)}) custom-call(f32[8,8,16,768]{3,2,1,0:T(8,128)} %init_ref.1, f32[3,768]{1,0:T(4,128)} %vel_in.1, f32[768]{0:T(1024)} %weight_in.1, s32[8,8,16]{2,1,0:T(8,128)} %wall_in.1, f32[8,8,16]{2,1,0:T(8,128)} %wall_temp_in.1, f32[1,1]{1,0:T(1,128)} %bitcast.1.target_ref), custom_call_target="tpu_custom_call" | custom-call | tf_op jit(solution)/shard_map/pallas_call | solution.py:605
  60.1 1.7 %copy.11 = f32[8,8,16,768]{3,2,1,0:T(8,128)} copy(f32[8,8,16,768]{3,2,1,0:T(8,128)S(1)} %get-tuple-element.4) | data formatting | bytes 6291456
  61.8 0.7 %copy.12 = f32[5,8,8,16]{3,2,1,0:T(8,128)} copy(f32[5,8,8,16]{3,2,1,0:T(8,128)S(1)} %get-tuple-element.5) | data formatting | bytes 40960
